TPU v7x, 32 devices: a whole 2x2x4 slice. The times are simulated.
32 devices in a mesh: leaf: 8 (over y, x, core), sub: 4 (over z).
Axes of the slice: x: 2, y: 2, z: 4, core: 2. Of those that a mesh axis runs over, the one named last changes fastest.
Arguments:
- charges: float32 [16, 64, 4, 8, 2048], P(None, None, 'sub', 'leaf'), may hold values from -6 to 6
- ordering: int32 [4, 8, 2048], P('sub', 'leaf'), may hold values from 0 to 2047, each once within a row
- jitter: float32 [3, 4, 8, 2048], P(None, 'sub', 'leaf'), may hold values from 0 to 1
- leaf_bases: float32 [4, 8, 64, 2048], P('sub', 'leaf'), may hold values from -0.125 to 0.125
- transfer: float32 [5, 2, 64, 64], replicated, may hold values from -0.5 to 0.5
- coupling: float32 [5, 2, 64, 64], replicated, may hold values from -0.75 to 0.75
Outputs:
- potential: float32 [16, 64, 4, 8, 2048], P(None, None, 'sub', 'leaf')
All inputs are finite; a program needn't handle non-finite values.
Results may differ from a plain program's by a relative error of at most 0.0003.
Values sent between devices are 32-bit elements; how exact they have to be, the bound alone decides.
No kernel may reach another device: no remote copies, remote signals or barrier semaphores. Data moves between devices by JAX's collectives and lax.ppermute only.
A program may use at most 128 MiB of HBM per device.

v0:
```python
import functools
import math

import jax
import jax.numpy as jnp
from jax import lax
from jax.experimental import pallas as pl
from jax.experimental.pallas import tpu as pltpu
from jax.sharding import PartitionSpec as P


DELTA_SQ = 0.0025
PRECISE = lax.Precision.HIGHEST
LANES = 128
ROWS = 256
GROUP = 512
TILE = 256
BF16 = jnp.bfloat16
F32 = jnp.float32
WIDE8 = jnp.float8_e5m2
FINE8 = jnp.float8_e4m3fn
LO_UP = 2.0**20
FULL_UP = 2.0**13
W_UP = 2.0**9
W_LO_UP = 2.0**16
NEAR_DOWN = 2.0**-29
BASE_UP = 2.0**10
MOMENT_DOWN = 2.0**-30


def dot(a, b):
    return jnp.dot(a, b, preferred_element_type=F32)


def split2(value):
    high = value.astype(BF16)
    return high, (value - high.astype(F32)).astype(BF16)


def strip_indices(order_ref, tail, width):
    count = order_ref.shape[1]
    return jnp.where(tail, order_ref[:, count - width :], order_ref[:, :width])


def strip_places(jitter_ref, tail, width, unit):
    count = jitter_ref.shape[2]

    def part(component):
        row = jitter_ref[component]
        return jnp.where(tail, row[:, count - width :], row[:, :width])

    start = jnp.where(tail, count - width, 0)
    index = (lax.broadcasted_iota(jnp.int32, (1, width), 1) + start).astype(F32)
    along = (index + part(0)) * (unit / count)
    return along, part(1) * unit, part(2) * unit


def stack_rows(rows, total):
    width = rows[0].shape[1]
    sublane = lax.broadcasted_iota(jnp.int32, (total, width), 0)
    result = jnp.zeros((total, width), F32)
    for position, row in enumerate(rows):
        result = jnp.where(sublane == position, row, result)
    return result


def fill_selector(index, wide_ref, fine_ref):
    count, width = wide_ref.shape
    for first in range(0, count, ROWS):
        row = lax.broadcasted_iota(jnp.int32, (ROWS, width), 0) + first
        hit = jnp.where(row == index, 1.0, 0.0)
        wide_ref[pl.ds(first, ROWS), :] = hit.astype(BF16)
        fine_ref[pl.ds(first, ROWS), :] = hit.astype(FINE8)


def cross_kernel(unit, order_ref, jitter_ref, x_ref, upper_ref, lower_ref, high_ref, low_ref, sel_ref, sel8_ref):
    step = pl.program_id(0)
    points = high_ref.shape[1]
    width = upper_ref.shape[1]
    rows = high_ref.shape[0]
    tail = (lax.axis_index("leaf") & 1) == 1

    @pl.when(step == 0)
    def _():
        fill_selector(strip_indices(order_ref, tail, width), sel_ref, sel8_ref)
        upper_ref[rows:, :] = stack_rows(strip_places(jitter_ref, tail, width, unit), 8)

    pieces = points // LANES
    for piece in range(pieces):
        value = x_ref[pl.ds(piece, rows, stride=pieces), :]
        high = value.astype(BF16)
        lanes = pl.ds(piece * LANES, LANES)
        high_ref[:, lanes] = high
        low_ref[:, lanes] = ((value - high.astype(F32)) * LO_UP).astype(WIDE8)
        low_ref[:, pl.ds(points + piece * LANES, LANES)] = (value * FULL_UP).astype(WIDE8)
    picked = dot(high_ref[...], sel_ref[...]) + dot(low_ref[:, :points], sel8_ref[...]) * (1.0 / LO_UP)

    @pl.when(step == 0)
    def _():
        upper_ref[:rows, :] = picked

    @pl.when(step == 1)
    def _():
        lower_ref[...] = picked


def places_kernel(unit, order_ref, jitter_ref, base_ref, spread_ref, base16_ref, base8_ref, far_ref, packed_ref):
    step = pl.program_id(0)
    points = order_ref.shape[1]
    rank = base_ref.shape[0]
    rows = base16_ref.shape[0]

    @pl.when(step == 0)
    def _():
        high, low = split2(base_ref[...])
        packed_ref[0:rank, :] = high
        packed_ref[rank : 2 * rank, :] = low
        index = lax.broadcasted_iota(jnp.int32, (1, points), 1).astype(F32)
        coords = [(index + jitter_ref[0]) * (unit / points), jitter_ref[1] * unit, jitter_ref[2] * unit]
        rest = coords
        pieces = []
        for _ in range(3):
            rounded = [r.astype(BF16).astype(F32) for r in rest]
            pieces.extend(rounded)
            rest = [r - q for r, q in zip(rest, rounded)]
        packed_ref[2 * rank : 2 * rank + 16, :] = stack_rows(pieces, 16).astype(BF16)
        packed_ref[2 * rank + 16 :, :] = jnp.zeros((2 * LANES - 2 * rank - 16, points), BF16)
        far_ref[0:rank, :] = high
        far_ref[rank : 2 * rank, :] = high
        far_ref[2 * rank : 3 * rank, :] = low
        far_ref[3 * rank :, :] = low

    row = lax.broadcasted_iota(jnp.int32, (rows, points), 0) + step * rows
    hit = jnp.where(row == order_ref[...], 1.0, 0.0).astype(BF16)
    moved = lax.dot_general(hit, packed_ref[...], (((1,), (1,)), ((), ())), preferred_element_type=F32)
    both = moved[:, :LANES]
    swap = pltpu.roll(both, LANES // 2, 1)
    left = lax.broadcasted_iota(jnp.int32, (rows, LANES), 1) < LANES // 2
    high = jnp.where(left, both, swap)
    low = jnp.where(left, swap, both)
    base16_ref[:, :LANES] = high.astype(BF16)
    base16_ref[:, LANES:] = low.astype(BF16)
    base8_ref[...] = (high * BASE_UP).astype(FINE8)
    place = moved[:, LANES:]
    place = place + pltpu.roll(place, LANES - 3, 1) + pltpu.roll(place, LANES - 6, 1)
    for component in range(3):
        spread_ref[component] = jnp.broadcast_to(place[:, component : component + 1], (rows, LANES))


def twice(block):
    wide = jnp.concatenate([block, block], axis=1)
    left = lax.broadcasted_iota(jnp.int32, wide.shape, 1) < block.shape[1]
    return jnp.concatenate([jnp.where(left, wide, 0.0), jnp.where(left, 0.0, wide)], axis=0)


def matrices_kernel(leaf_levels, transfer_ref, coupling_ref, lift_ref, couple_ref):
    levels = transfer_ref.shape[0]
    leaf = lax.axis_index("leaf")
    sub = lax.axis_index("sub")
    down = None
    span = 2 * transfer_ref.shape[2]
    for level in range(levels):
        bit = leaf >> level & 1 if level < leaf_levels else sub >> (level - leaf_levels) & 1
        right = bit == 1
        first, second = transfer_ref[level, 0], transfer_ref[level, 1]
        own = jnp.where(right, second, first)
        other = jnp.where(right, first, second)
        couple = jnp.where(right, coupling_ref[level, 1], coupling_ref[level, 0]).T
        if down is not None:
            couple = jnp.dot(couple, down, precision=PRECISE, preferred_element_type=F32)
        high, low = split2(twice(couple))
        couple_ref[pl.ds(level * span, span), :] = high
        couple_ref[pl.ds((levels + level) * span, span), :] = high
        couple_ref[pl.ds((2 * levels + level) * span, span), :] = low
        if level < levels - 1:
            down = own.T if down is None else jnp.dot(own.T, down, precision=PRECISE, preferred_element_type=F32)
            own_high, own_low = split2(twice(own))
            other_high, other_low = split2(twice(other))
            for position, part in enumerate((own_high, other_high, own_high, other_high, own_low, other_low)):
                lift_ref[level, pl.ds(position * span, span), :] = part


def core_kernel(unit, order_ref, jitter_ref, base16_ref, base8_ref, high_ref, low_ref, strip_ref, sel_ref, sel8_ref):
    count, points = high_ref.shape
    width = sel_ref.shape[1]
    tail = (lax.axis_index("leaf") & 1) == 0
    fill_selector(strip_indices(order_ref, tail, width), sel_ref, sel8_ref)
    strip_ref[count:, :width] = stack_rows(strip_places(jitter_ref, tail, width, unit), 8)
    strip_ref[count // 2 :, width:] = jnp.zeros((count // 2 + 8, LANES), F32)
    high = high_ref[...]
    low = low_ref[:, :points]
    moment = dot(high, base16_ref[...])
    moment = moment[:, :LANES] + moment[:, LANES:] + dot(low, base8_ref[...]) * MOMENT_DOWN
    half = GROUP // 2
    left = lax.broadcasted_iota(jnp.int32, (half, LANES), 1) < LANES // 2
    for group in range(count // GROUP):
        first = group * GROUP
        packed = jnp.where(left, moment[first : first + half], moment[first + half : first + GROUP])
        strip_ref[group * half : (group + 1) * half, width:] = packed
    strip_ref[:count, :width] = dot(high, sel_ref[...]) + dot(low, sel8_ref[...]) * (1.0 / LO_UP)


def lift_kernel(own_ref, other_ref, matrix_ref, out_ref):
    own_high, own_low = split2(own_ref[...])
    other_high, other_low = split2(other_ref[...])
    stacked = jnp.concatenate([own_high, other_high, own_low, other_low, own_high, other_high], axis=1)
    out_ref[...] = dot(stacked, matrix_ref[0])


def target_places(jitter_ref, unit, place_ref):
    points = jitter_ref.shape[2]
    index = lax.broadcasted_iota(jnp.int32, (1, points), 1).astype(F32)
    rows = [(index + jitter_ref[0]) * (unit / points), jitter_ref[1] * unit, jitter_ref[2] * unit]
    place_ref[...] = stack_rows(rows, 8)


def fill_weights(unit, place_ref, spread_ref, high_ref, fine_ref, columns, sources):
    root = unit * math.sqrt(DELTA_SQ)
    for block in range(0, sources, ROWS):
        here = pl.ds(block, ROWS)
        for part in range(TILE // LANES):
            lanes = pl.ds(part * LANES, LANES)
            square = root * root
            for component in range(3):
                there = place_ref[component : component + 1, pl.ds(columns + part * LANES, LANES)]
                gap = spread_ref[component, here, :] - there
                square = gap * gap + square
            store_weight(square, high_ref, fine_ref, here, pl.ds(sources + block, ROWS), lanes)


def own_kernel(unit, tiles, chunk, jitter_ref, spread_ref, high_ref, low_ref, *refs):
    out_ref, place_ref, ha, wa, hb, wb = refs[-6:]
    points = high_ref.shape[1]
    target_places(jitter_ref, unit, place_ref)
    buffers = ((ha, wa), (hb, wb))

    def fill(tile):
        high, fine = buffers[tile % 2]
        fill_weights(unit, place_ref, spread_ref, high, fine, (chunk * tiles + tile) * TILE, points)

    fill(0)
    for tile in range(tiles):
        if tile + 1 < tiles:
            fill(tile + 1)
        high, fine = buffers[tile % 2]
        out_ref[chunk, :, tile * TILE : (tile + 1) * TILE] = (
            dot(high_ref[...], high[...]) + dot(low_ref[...], fine[...]) * NEAR_DOWN
        )


def store_weight(square, high_ref, fine_ref, here, there, lanes):
    weight = lax.rsqrt(square)
    high = weight.astype(BF16)
    high_ref[here, lanes] = high
    fine_ref[here, lanes] = (weight * W_UP).astype(FINE8)
    fine_ref[there, lanes] = ((weight - high.astype(F32)) * W_LO_UP).astype(FINE8)


def final_kernel(unit, levels, *refs):
    jitter_ref, core_ref, upper_ref, lower_ref = refs[:4]
    sib_refs = refs[4 : 4 + levels]
    couple_ref, far_ref = refs[4 + levels : 6 + levels]
    near_ref, out_ref, left_ref, low_ref, spread_ref, place_ref, ha, wa, hb, wb, stage_ref, sems = refs[6 + levels :]
    chunks, count, _ = near_ref.shape
    width = upper_ref.shape[1]
    sources = 2 * width

    def fill(tile, high, fine):
        columns = pl.multiple_of(tile * TILE, TILE)
        fill_weights(unit, place_ref, spread_ref, high, fine, columns, sources)
        high[sources:, :] = far_ref[:, pl.ds(columns, TILE)]

    target_places(jitter_ref, unit, place_ref)
    odd = (lax.axis_index("leaf") & 1) == 1
    sign = jnp.where(odd, unit, -unit)

    def place_strip(position, across, shift):
        lanes = pl.ds(position * width, width)
        for component in range(3):
            column = across[:, component : component + 1]
            if component == 0:
                column = column + shift
            spread_ref[component, lanes, :] = jnp.broadcast_to(column, (width, LANES))

    def take_strip(position, rows, value):
        high = value.astype(BF16)
        lanes = pl.ds(position * width, width)
        left_ref[rows, lanes] = high
        low_ref[rows, lanes] = ((value - high.astype(F32)) * LO_UP).astype(WIDE8)
        low_ref[rows, pl.ds(sources + position * width, width)] = (value * FULL_UP).astype(WIDE8)

    place_strip(0, core_ref[count:, :width].T, -sign)
    place_strip(1, upper_ref[count // 2 :, :].T, sign)
    fill(0, ha, wa)
    take_strip(0, pl.ds(0, count), core_ref[:count, :width])
    take_strip(1, pl.ds(0, count // 2), upper_ref[: count // 2, :])
    take_strip(1, pl.ds(count // 2, count // 2), lower_ref[...])
    parts = [split2(sib_refs[0][: count // 2, width:])] + [split2(ref[...]) for ref in sib_refs[1:]]
    stacked = jnp.concatenate([p[0] for p in parts] + [p[1] for p in parts] + [p[0] for p in parts], axis=1)
    expansion = dot(stacked, couple_ref[...])
    high = expansion.astype(BF16).astype(F32)
    low = pltpu.roll(expansion - high, LANES // 2, 1)
    half = GROUP // 2
    is_left = lax.broadcasted_iota(jnp.int32, (half, LANES), 1) < LANES // 2
    for block in range(count // GROUP):
        h = high[block * half : (block + 1) * half]
        l = low[block * half : (block + 1) * half]
        upper = pl.ds(block * GROUP, half)
        lower = pl.ds(block * GROUP + half, half)
        left_ref[upper, sources : sources + LANES] = jnp.where(is_left, h, l).astype(BF16)
        left_ref[lower, sources : sources + LANES] = jnp.where(is_left, l, h).astype(BF16)
        left_ref[upper, sources + LANES :] = jnp.where(is_left, h, 0.0).astype(BF16)
        left_ref[lower, sources + LANES :] = jnp.where(is_left, 0.0, h).astype(BF16)

    parts_per_tile = TILE // LANES

    def copy(pair, tile):
        slot = 2 * (pair % 2) + tile
        lanes = pl.ds((2 * pair + tile) * parts_per_tile, parts_per_tile)
        return pltpu.make_async_copy(
            stage_ref.at[slot].reshape(count, parts_per_tile, LANES), out_ref.at[:, lanes, :], sems.at[slot]
        )

    def product(pair, tile, h, w):
        lanes = slice(tile * TILE, (tile + 1) * TILE)
        value = near_ref[pair, :, lanes] + dot(left_ref[...], h[...]) + dot(low_ref[...], w[...]) * NEAR_DOWN
        for part in range(parts_per_tile):
            stage_ref[2 * (pair % 2) + tile, pl.ds(part, count, stride=parts_per_tile), :] = value[
                :, part * LANES : (part + 1) * LANES
            ]

    def run(pair, carry):
        @pl.when(pair >= 2)
        def _():
            copy(pair - 2, 0).wait()
            copy(pair - 2, 1).wait()

        fill(2 * pair + 1, hb, wb)
        product(pair, 0, ha, wa)
        copy(pair, 0).start()
        fill(jnp.minimum(2 * pair + 2, 2 * chunks - 1), ha, wa)
        product(pair, 1, hb, wb)
        copy(pair, 1).start()
        return carry

    lax.fori_loop(0, chunks, run, 0)
    for pair in range(chunks - 2, chunks):
        copy(pair, 0).wait()
        copy(pair, 1).wait()


def cost(flops, moved):
    return pl.CostEstimate(flops=int(flops), bytes_accessed=int(moved), transcendentals=0)


def whole(array):
    rank = len(array.shape)
    return pl.BlockSpec(array.shape, lambda *_: (0,) * rank)


def shape(dims, dtype=F32):
    return jax.ShapeDtypeStruct(dims, dtype)


def body(charges, ordering, jitter, leaf_bases, transfer, coupling):
    points = charges.shape[4]
    count = charges.shape[0] * charges.shape[1]
    width = points // 4
    rank = leaf_bases.shape[2]
    unit = math.sqrt(points)
    leaf_count = lax.axis_size("leaf")
    sub_count = lax.axis_size("sub")
    leaf_levels = leaf_count.bit_length() - 1
    sub_levels = sub_count.bit_length() - 1
    levels = leaf_levels + sub_levels
    half = count // 2
    pieces = points // LANES
    x = charges.reshape(count * pieces, LANES)
    order = ordering.reshape(1, points)
    offsets = jitter.reshape(3, 1, points)
    base = leaf_bases.reshape(rank, points)
    params = lambda mib: pltpu.CompilerParams(vmem_limit_bytes=mib << 20)
    vmem = pl.BlockSpec(memory_space=pltpu.VMEM)

    upper, lower, high, low = pl.pallas_call(
        functools.partial(cross_kernel, unit),
        grid=(2,),
        in_specs=[whole(order), whole(offsets), pl.BlockSpec((half * pieces, LANES), lambda i: (i, 0))],
        out_specs=[
            pl.BlockSpec((half + 8, width), lambda i: (0, 0)),
            pl.BlockSpec((half, width), lambda i: (0, 0)),
            pl.BlockSpec((half, points), lambda i: (i, 0)),
            pl.BlockSpec((half, 2 * points), lambda i: (i, 0)),
        ],
        out_shape=[
            shape((half + 8, width)),
            shape((half, width)),
            shape((count, points), BF16),
            shape((count, 2 * points), WIDE8),
        ],
        scratch_shapes=[pltpu.VMEM((points, width), BF16), pltpu.VMEM((points, width), FINE8)],
        compiler_params=params(30),
        cost_estimate=cost(3 * count * points * width, 16 * count * points),
        name="cross",
    )(order, offsets, pltpu.with_memory_space_constraint(x, pltpu.HBM))
    last = leaf_count - 1
    middle = leaf_count // 2
    up_pairs = [(i, i + 1) for i in range(1, last, 2)]
    direct = up_pairs + [(b, a) for a, b in up_pairs]
    ends = (0, middle - 1, middle, last)
    to_relay = [(middle - 1, last), (middle, 0)] + [(i, i) for i in range(leaf_count) if i not in ends]
    relayed = [p for p in direct if p[0] not in ends] + [(last, middle), (0, middle - 1)]
    if leaf_count < 4:
        to_relay, relayed = [], []
    upper_in = lax.ppermute(upper, "leaf", direct)
    relay = lax.ppermute(lower, "leaf", to_relay)

    spread, base16, base8, far = pl.pallas_call(
        functools.partial(places_kernel, unit),
        grid=(points // GROUP,),
        in_specs=[whole(order), whole(offsets), whole(base)],
        out_specs=[
            pl.BlockSpec((3, GROUP, LANES), lambda i: (0, i, 0)),
            pl.BlockSpec((GROUP, 2 * LANES), lambda i: (i, 0)),
            pl.BlockSpec((GROUP, LANES), lambda i: (i, 0)),
            pl.BlockSpec((4 * rank, points), lambda i: (0, 0)),
        ],
        out_shape=[
            shape((3, points, LANES)),
            shape((points, 2 * LANES), BF16),
            shape((points, LANES), FINE8),
            shape((4 * rank, points), BF16),
        ],
        scratch_shapes=[pltpu.VMEM((2 * LANES, points), BF16)],
        compiler_params=params(16),
        cost_estimate=cost(2 * points * points * 256, 5 * points * 1024),
        name="places",
    )(order, offsets, base)

    core = pl.pallas_call(
        functools.partial(core_kernel, unit),
        in_specs=[vmem] * 6,
        out_specs=vmem,
        out_shape=shape((count + 8, width + LANES)),
        scratch_shapes=[pltpu.VMEM((points, width), BF16), pltpu.VMEM((points, width), FINE8)],
        compiler_params=params(16),
        cost_estimate=cost(3 * count * points * (width + 256), 6 * count * points),
        name="core",
    )(order, offsets, base16, base8, high, low)
    core_in = lax.ppermute(core, "leaf", [(i, i ^ 1) for i in range(leaf_count)])

    lift, couple = pl.pallas_call(
        functools.partial(matrices_kernel, leaf_levels),
        in_specs=[vmem] * 2,
        out_specs=[vmem] * 2,
        out_shape=[shape((levels - 1, 12 * rank, 2 * rank), BF16), shape((6 * levels * rank, 2 * rank), BF16)],
        compiler_params=params(8),
        cost_estimate=cost(1e6, 1e6),
        name="matrices",
    )(transfer, coupling)

    tiles = 2
    chunks = points // (tiles * TILE)
    near = None

    def own(chunk, near):
        operands = (offsets, spread, high, low) + (() if near is None else (near,))
        return pl.pallas_call(
            functools.partial(own_kernel, unit, tiles, chunk),
            in_specs=[vmem] * 4 + ([] if near is None else [pl.BlockSpec(memory_space=pl.ANY)]),
            out_specs=vmem,
            out_shape=shape((chunks, count, tiles * TILE)),
            scratch_shapes=[pltpu.VMEM((8, points), F32)]
            + [pltpu.VMEM((points, TILE), BF16), pltpu.VMEM((2 * points, TILE), FINE8)] * 2,
            input_output_aliases={} if near is None else {4: 0},
            compiler_params=params(12),
            cost_estimate=cost(4 * count * points * tiles * TILE, 10 * count * points),
        )(*operands)

    def lifted(level, own_moment, other, from_strip):
        spec = pl.BlockSpec((half, LANES), (lambda i: (0, width // LANES)) if from_strip else (lambda i: (0, 0)))
        return pl.pallas_call(
            lift_kernel,
            grid=(1,),
            in_specs=[spec, spec, pl.BlockSpec((1, 12 * rank, 2 * rank), lambda i: (level, 0, 0))],
            out_specs=pl.BlockSpec((half, LANES), lambda i: (0, 0)),
            out_shape=shape((half, LANES)),
            compiler_params=params(8),
            cost_estimate=cost(2 * half * 768 * 128, 3 * half * 512),
        )(own_moment, other, lift)

    near = own(0, None)
    siblings = [core_in]
    current = core
    for level in range(1, levels):
        current = lifted(level - 1, current, siblings[-1], level == 1)
        axis, bit = ("leaf", level) if level < leaf_levels else ("sub", level - leaf_levels)
        pairs = [(i, i ^ 1 << bit) for i in range(lax.axis_size(axis))]
        siblings.append(lax.ppermute(current, axis, pairs))
        if level == 1:
            lower_in = lax.ppermute(relay, "leaf", relayed)
        if level < chunks:
            near = own(level, near)
    for chunk in range(levels, chunks):
        near = own(chunk, near)

    sources = 2 * width
    out = pl.pallas_call(
        functools.partial(final_kernel, unit, levels),
        in_specs=[vmem] * (7 + levels),
        out_specs=pl.BlockSpec(memory_space=pl.ANY),
        out_shape=shape((count, pieces, LANES)),
        scratch_shapes=[
            pltpu.VMEM((count, sources + 4 * rank), BF16),
            pltpu.VMEM((count, 2 * sources), WIDE8),
            pltpu.VMEM((3, sources, LANES), F32),
            pltpu.VMEM((8, points), F32),
        ]
        + [pltpu.VMEM((sources + 4 * rank, TILE), BF16), pltpu.VMEM((2 * sources, TILE), FINE8)] * 2
        + [pltpu.VMEM((4, count * TILE // LANES, LANES), F32), pltpu.SemaphoreType.DMA((4,))],
        compiler_params=params(24),
        cost_estimate=cost(4 * count * points * sources, 8 * count * points),
        name="final",
    )(offsets, core_in, upper_in, lower_in, *siblings, couple, far, near)
    return out.reshape(charges.shape)


def solution(mesh):
    in_specs = (
        P(None, None, "sub", "leaf", None),
        P("sub", "leaf", None),
        P(None, "sub", "leaf", None),
        P("sub", "leaf", None, None),
        P(),
        P(),
    )
    out_specs = P(None, None, "sub", "leaf", None)

    return jax.shard_map(body, mesh=mesh, in_specs=in_specs, out_specs=out_specs, check_vma=False)
```

profile of v0, /device:TPU:0, one launch (start us, length us, event | category | flops | bytes accessed | tf_op | source)
XLA Modules:
  0.0 106.4 jit_solution(17163226775617278986)
XLA Ops:
  0.0 0.7 copy-done
  0.7 0.7 copy-done.5
  1.4 9.1 %cross.1 = (f32[520,512]{1,0:T(8,128)S(1)}, f32[512,512]{1,0:T(8,128)S(1)}, bf16[1024,2048]{1,0:T(8,128)(2,1)S(1)}, f8e5m2[1024,4096]{1,0:T(32,128)(4,1)S(1)}) custom-call(s32[1,2048]{1,0:T(1,128)S(1)} %bitcast.14, f32[3,1,2048]{2,1,0:T(1,128)S(1)} %bitcast.5, f32[16384,128]{1,0:T(8,128)} %bitcast.17), custom_call_target="tpu_custom_call" | custom-call | flops 3221225472 | bytes 33554432 | tf_op jit(solution)/shard_map/cross/pallas_call | solution.py:385
  10.5 5.1 %places.1 = (f32[3,2048,128]{2,1,0:T(8,128)S(1)}, bf16[2048,256]{1,0:T(8,128)(2,1)S(1)}, f8e4m3fn[2048,128]{1,0:T(32,128)(4,1)S(1)}, bf16[256,2048]{1,0:T(8,128)(2,1)S(1)}) custom-call(s32[1,2048]{1,0:T(1,128)S(1)} %bitcast.15, f32[3,1,2048]{2,1,0:T(1,128)S(1)} %bitcast.6, f32[64,2048]{1,0:T(8,128)S(1)} %bitcast.13), custom_call_target="tpu_custom_call" | custom-call | flops 2147483648 | bytes 10485760 | tf_op jit(solution)/shard_map/places/pallas_call | solution.py:418
  15.6 0.0 copy-start.2
  15.7 0.0 copy-start.3
  15.7 5.1 %core.1.own_ref = f32[1032,640]{1,0:T(8,128)S(1)} custom-call(s32[1,2048]{1,0:T(1,128)S(1)} %bitcast.16, f32[3,1,2048]{2,1,0:T(1,128)S(1)} %bitcast.7, bf16[2048,256]{1,0:T(8,128)(2,1)S(1)} %get-tuple-element.15.base16_ref, f8e4m3fn[2048,128]{1,0:T(32,128)(4,1)S(1)} %get-tuple-element.16.base8_ref, bf16[1024,2048]{1,0:T(8,128)(2,1)S(1)} %get-tuple-element.17.high_ref, ...), custom_call_target="tpu_custom_call" | custom-call | flops 4831838208 | bytes 12582912 | tf_op jit(solution)/shard_map/core/pallas_call | solution.py:440
  20.8 0.0 copy-start.1
  20.8 0.6 collective-permute-start
  21.3 1.3 %collective-permute-start.2 = (f32[512,512]{1,0:T(8,128)S(1)}, f32[512,512]{1,0:T(8,128)S(1)}, u32[]{:S(2)}, u32[]{:S(2)}) collective-permute-start(f32[512,512]{1,0:T(8,128)S(1)} %get-tuple-element.20), channel_id=1, source_target_pairs={{12,28},{16,0},{4,4},{8,8},{20,20},{24,24},{13,29},{17,1},{5,5},{9... | collective-permute-start | bytes 3145736 | tf_op jit(solution)/shard_map/ppermute | solution.py:416
  22.6 0.9 collective-permute-start.1
  23.6 0.9 matrices.1
  24.5 1.4 %collective-permute-done.other_ref.refs_1_.refs_4_ = f32[1032,640]{1,0:T(8,128)S(1)} collective-permute-done((f32[1032,640]{1,0:T(8,128)S(1)}, f32[1032,640]{1,0:T(8,128)S(1)}, u32[]{:S(2)}, u32[]{:S(2)}) %collective-permute-start) | collective-permute-done | bytes 2641952 | tf_op jit(solution)/shard_map/ppermute | solution.py:450
  25.9 0.4 shard_map.64.own_ref
  26.3 2.9 %collective-permute-start.4 = (f32[512,128]{1,0:T(8,128)S(1)}, f32[512,128]{1,0:T(8,128)S(1)}, u32[]{:S(2)}, u32[]{:S(2)}) collective-permute-start(f32[512,128]{1,0:T(8,128)S(1)} %shard_map.64.own_ref), channel_id=1, source_target_pairs={{0,8},{4,12},{8,0},{12,4},{16,24},{20,28},{24,16},{28,20},{1,9},{5... | collective-permute-start | bytes 786440 | tf_op jit(solution)/shard_map/ppermute | solution.py:499
  29.2 5.2 %shard_map.68.refs_0_ = f32[4,1024,512]{2,1,0:T(8,128)S(1)} custom-call(f32[3,1,2048]{2,1,0:T(1,128)S(1)} %bitcast.8, f32[3,2048,128]{2,1,0:T(8,128)S(1)} %get-tuple-element.24.spread_ref, bf16[1024,2048]{1,0:T(8,128)(2,1)S(1)} %get-tuple-element.17.high_ref, f8e5m2[1024,4096]{1,0:T(32,128)(4,1)S(1)} %get-tuple-element.18.low_ref), custom_call_target="tpu_custom_call" | custom-call | flops 4294967296 | bytes 20971520 | tf_op jit(solution)/shard_map/pallas_call | solution.py:468
  34.4 3.6 %collective-permute-done.2 = f32[512,512]{1,0:T(8,128)S(1)} collective-permute-done((f32[512,512]{1,0:T(8,128)S(1)}, f32[512,512]{1,0:T(8,128)S(1)}, u32[]{:S(2)}, u32[]{:S(2)}) %collective-permute-start.2) | collective-permute-done | bytes 1048608 | tf_op jit(solution)/shard_map/ppermute | solution.py:416
  38.0 2.7 %collective-permute-start.3 = (f32[512,512]{1,0:T(8,128)S(1)}, f32[512,512]{1,0:T(8,128)S(1)}, u32[]{:S(2)}, u32[]{:S(2)}) collective-permute-start(f32[512,512]{1,0:T(8,128)S(1)} %collective-permute-done.2), channel_id=1, source_target_pairs={{4,8},{20,24},{8,4},{24,20},{28,16},{0,12},{5,9},{21,25},{9,5},{25... | collective-permute-start | bytes 3145736 | tf_op jit(solution)/shard_map/ppermute | solution.py:501
  40.8 13.4 %collective-permute-done.4.other_ref.refs_5_ = f32[512,128]{1,0:T(8,128)S(1)} collective-permute-done((f32[512,128]{1,0:T(8,128)S(1)}, f32[512,128]{1,0:T(8,128)S(1)}, u32[]{:S(2)}, u32[]{:S(2)}) %collective-permute-start.4) | collective-permute-done | bytes 262176 | tf_op jit(solution)/shard_map/ppermute | solution.py:499
  54.2 0.4 shard_map.65.own_ref
  54.5 5.9 %collective-permute-start.5 = (f32[512,128]{1,0:T(8,128)S(1)}, f32[512,128]{1,0:T(8,128)S(1)}, u32[]{:S(2)}, u32[]{:S(2)}) collective-permute-start(f32[512,128]{1,0:T(8,128)S(1)} %shard_map.65.own_ref), channel_id=1, source_target_pairs={{0,16},{4,20},{8,24},{12,28},{16,0},{20,4},{24,8},{28,12},{1,17},{... | collective-permute-start | bytes 786440 | tf_op jit(solution)/shard_map/ppermute | solution.py:499
  60.5 5.2 %shard_map.69.refs_0_ = f32[4,1024,512]{2,1,0:T(8,128)S(1)} custom-call(f32[3,1,2048]{2,1,0:T(1,128)S(1)} %bitcast.9, f32[3,2048,128]{2,1,0:T(8,128)S(1)} %get-tuple-element.24.spread_ref, bf16[1024,2048]{1,0:T(8,128)(2,1)S(1)} %get-tuple-element.17.high_ref, f8e5m2[1024,4096]{1,0:T(32,128)(4,1)S(1)} %get-tuple-element.18.low_ref, ...), custom_call_target="tpu_custom_call", output_to_operand_aliasing={{}: (4, {})} | custom-call | flops 4294967296 | bytes 20971520 | tf_op jit(solution)/shard_map/pallas_call | solution.py:468
  65.7 1.5 %collective-permute-done.5.other_ref.refs_6_ = f32[512,128]{1,0:T(8,128)S(1)} collective-permute-done((f32[512,128]{1,0:T(8,128)S(1)}, f32[512,128]{1,0:T(8,128)S(1)}, u32[]{:S(2)}, u32[]{:S(2)}) %collective-permute-start.5) | collective-permute-done | bytes 262176 | tf_op jit(solution)/shard_map/ppermute | solution.py:499
  67.2 0.4 shard_map.66.own_ref
  67.6 2.0 %collective-permute-start.6 = (f32[512,128]{1,0:T(8,128)S(1)}, f32[512,128]{1,0:T(8,128)S(1)}, u32[]{:S(2)}, u32[]{:S(2)}) collective-permute-start(f32[512,128]{1,0:T(8,128)S(1)} %shard_map.66.own_ref), channel_id=1, source_target_pairs={{0,1},{1,0},{2,3},{3,2},{4,5},{5,4},{6,7},{7,6},{8,9},{9,8},{10,11... | collective-permute-start | bytes 786440 | tf_op jit(solution)/shard_map/ppermute | solution.py:499
  69.6 5.2 %shard_map.70.refs_0_ = f32[4,1024,512]{2,1,0:T(8,128)S(1)} custom-call(f32[3,1,2048]{2,1,0:T(1,128)S(1)} %bitcast.10, f32[3,2048,128]{2,1,0:T(8,128)S(1)} %get-tuple-element.24.spread_ref, bf16[1024,2048]{1,0:T(8,128)(2,1)S(1)} %get-tuple-element.17.high_ref, f8e5m2[1024,4096]{1,0:T(32,128)(4,1)S(1)} %get-tuple-element.18.low_ref, ...), custom_call_target="tpu_custom_call", output_to_operand_aliasing={{}: (4, {})} | custom-call | flops 4294967296 | bytes 20971520 | tf_op jit(solution)/shard_map/pallas_call | solution.py:468
  74.8 1.3 %collective-permute-done.6.other_ref.refs_7_ = f32[512,128]{1,0:T(8,128)S(1)} collective-permute-done((f32[512,128]{1,0:T(8,128)S(1)}, f32[512,128]{1,0:T(8,128)S(1)}, u32[]{:S(2)}, u32[]{:S(2)}) %collective-permute-start.6) | collective-permute-done | bytes 262176 | tf_op jit(solution)/shard_map/ppermute | solution.py:499
  76.1 0.4 shard_map.67
  76.5 2.8 %collective-permute-start.7 = (f32[512,128]{1,0:T(8,128)S(1)}, f32[512,128]{1,0:T(8,128)S(1)}, u32[]{:S(2)}, u32[]{:S(2)}) collective-permute-start(f32[512,128]{1,0:T(8,128)S(1)} %shard_map.67), channel_id=1, source_target_pairs={{0,2},{1,3},{2,0},{3,1},{4,6},{5,7},{6,4},{7,5},{8,10},{9,11},{10,... | collective-permute-start | bytes 786440 | tf_op jit(solution)/shard_map/ppermute | solution.py:499
  79.3 5.5 %shard_map.71.refs_11_ = f32[4,1024,512]{2,1,0:T(8,128)S(1)} custom-call(f32[3,1,2048]{2,1,0:T(1,128)S(1)} %bitcast.11, f32[3,2048,128]{2,1,0:T(8,128)S(1)} %get-tuple-element.24.spread_ref, bf16[1024,2048]{1,0:T(8,128)(2,1)S(1)} %get-tuple-element.17.high_ref, f8e5m2[1024,4096]{1,0:T(32,128)(4,1)S(1)} %get-tuple-element.18.low_ref, ...), custom_call_target="tpu_custom_call", output_to_operand_aliasing={{}: (4, {})} | custom-call | flops 4294967296 | bytes 20971520 | tf_op jit(solution)/shard_map/pallas_call | solution.py:468
  84.8 5.9 %collective-permute-done.7.refs_8_ = f32[512,128]{1,0:T(8,128)S(1)} collective-permute-done((f32[512,128]{1,0:T(8,128)S(1)}, f32[512,128]{1,0:T(8,128)S(1)}, u32[]{:S(2)}, u32[]{:S(2)}) %collective-permute-start.7) | collective-permute-done | bytes 262176 | tf_op jit(solution)/shard_map/ppermute | solution.py:499
  90.7 15.5 %final.1 = f32[1024,16,128]{2,1,0:T(8,128)} custom-call(f32[3,1,2048]{2,1,0:T(1,128)S(1)} %bitcast.12, f32[1032,640]{1,0:T(8,128)S(1)} %collective-permute-done.other_ref.refs_1_.refs_4_, f32[520,512]{1,0:T(8,128)S(1)} %collective-permute-done.1.refs_2_, f32[512,512]{1,0:T(8,128)S(1)} %collective-permute-done.3.refs_3_, ...), custom_call_target="tpu_custom_call" | custom-call | flops 8589934592 | bytes 16777216 | tf_op jit(solution)/shard_map/final/pallas_call | solution.py:508
  (9 shorter events, 0.0 us)
Async XLA Ops:
  0.0 0.7 copy-start
  0.7 0.7 copy-start.5
  1.4 9.1 %copy-start.4 = (f32[1,1,64,2048]{3,2,1,0:T(8,128)S(1)}, f32[1,1,64,2048]{3,2,1,0:T(8,128)}, u32[]{:S(2)}) copy-start(f32[1,1,64,2048]{3,2,1,0:T(8,128)} %param.9) | copy-start | bytes 1572868
  15.6 7.9 %copy-start.2 = (f32[5,2,64,64]{3,2,1,0:T(8,128)S(1)}, f32[5,2,64,64]{3,2,1,0:T(8,128)}, u32[]{:S(2)}) copy-start(f32[5,2,64,64]{3,2,1,0:T(8,128)} %transfer_ref.1) | copy-start | bytes 491524
  15.7 7.9 %copy-start.3 = (f32[5,2,64,64]{3,2,1,0:T(8,128)S(1)}, f32[5,2,64,64]{3,2,1,0:T(8,128)}, u32[]{:S(2)}) copy-start(f32[5,2,64,64]{3,2,1,0:T(8,128)} %coupling_ref.1) | copy-start | bytes 491524
  20.8 8.4 %copy-start.1 = (f32[3,1,1,2048]{3,2,1,0:T(1,128)S(1)}, f32[3,1,1,2048]{3,2,1,0:T(1,128)}, u32[]{:S(2)}) copy-start(f32[3,1,1,2048]{3,2,1,0:T(1,128)} %param.8) | copy-start | bytes 73732
  20.8 5.1 %collective-permute-start = (f32[1032,640]{1,0:T(8,128)S(1)}, f32[1032,640]{1,0:T(8,128)S(1)}, u32[]{:S(2)}, u32[]{:S(2)}) collective-permute-start(f32[1032,640]{1,0:T(8,128)S(1)} %core.1.own_ref), channel_id=1, source_target_pairs={{0,4},{4,0},{8,12},{12,8},{16,20},{20,16},{24,28},{28,24},{1,5},{5... | collective-permute-start | bytes 7925768 | tf_op jit(solution)/shard_map/ppermute | solution.py:450
  21.3 16.7 %collective-permute-start.2 = (f32[512,512]{1,0:T(8,128)S(1)}, f32[512,512]{1,0:T(8,128)S(1)}, u32[]{:S(2)}, u32[]{:S(2)}) collective-permute-start(f32[512,512]{1,0:T(8,128)S(1)} %get-tuple-element.20), channel_id=1, source_target_pairs={{12,28},{16,0},{4,4},{8,8},{20,20},{24,24},{13,29},{17,1},{5,5},{9... | collective-permute-start | bytes 3145736 | tf_op jit(solution)/shard_map/ppermute | solution.py:416
  22.6 62.2 %collective-permute-start.1 = (f32[520,512]{1,0:T(8,128)S(1)}, f32[520,512]{1,0:T(8,128)S(1)}, u32[]{:S(2)}, u32[]{:S(2)}) collective-permute-start(f32[520,512]{1,0:T(8,128)S(1)} %get-tuple-element.19), channel_id=1, source_target_pairs={{4,8},{12,16},{20,24},{8,4},{16,12},{24,20},{5,9},{13,17},{21,25},... | collective-permute-start | bytes 3194888 | tf_op jit(solution)/shard_map/ppermute | solution.py:415
  26.3 27.9 %collective-permute-start.4 = (f32[512,128]{1,0:T(8,128)S(1)}, f32[512,128]{1,0:T(8,128)S(1)}, u32[]{:S(2)}, u32[]{:S(2)}) collective-permute-start(f32[512,128]{1,0:T(8,128)S(1)} %shard_map.64.own_ref), channel_id=1, source_target_pairs={{0,8},{4,12},{8,0},{12,4},{16,24},{20,28},{24,16},{28,20},{1,9},{5... | collective-permute-start | bytes 786440 | tf_op jit(solution)/shard_map/ppermute | solution.py:499
  38.0 46.8 %collective-permute-start.3 = (f32[512,512]{1,0:T(8,128)S(1)}, f32[512,512]{1,0:T(8,128)S(1)}, u32[]{:S(2)}, u32[]{:S(2)}) collective-permute-start(f32[512,512]{1,0:T(8,128)S(1)} %collective-permute-done.2), channel_id=1, source_target_pairs={{4,8},{20,24},{8,4},{24,20},{28,16},{0,12},{5,9},{21,25},{9,5},{25... | collective-permute-start | bytes 3145736 | tf_op jit(solution)/shard_map/ppermute | solution.py:501
  54.5 12.7 %collective-permute-start.5 = (f32[512,128]{1,0:T(8,128)S(1)}, f32[512,128]{1,0:T(8,128)S(1)}, u32[]{:S(2)}, u32[]{:S(2)}) collective-permute-start(f32[512,128]{1,0:T(8,128)S(1)} %shard_map.65.own_ref), channel_id=1, source_target_pairs={{0,16},{4,20},{8,24},{12,28},{16,0},{20,4},{24,8},{28,12},{1,17},{... | collective-permute-start | bytes 786440 | tf_op jit(solution)/shard_map/ppermute | solution.py:499
  67.6 8.6 %collective-permute-start.6 = (f32[512,128]{1,0:T(8,128)S(1)}, f32[512,128]{1,0:T(8,128)S(1)}, u32[]{:S(2)}, u32[]{:S(2)}) collective-permute-start(f32[512,128]{1,0:T(8,128)S(1)} %shard_map.66.own_ref), channel_id=1, source_target_pairs={{0,1},{1,0},{2,3},{3,2},{4,5},{5,4},{6,7},{7,6},{8,9},{9,8},{10,11... | collective-permute-start | bytes 786440 | tf_op jit(solution)/shard_map/ppermute | solution.py:499
  76.5 14.2 %collective-permute-start.7 = (f32[512,128]{1,0:T(8,128)S(1)}, f32[512,128]{1,0:T(8,128)S(1)}, u32[]{:S(2)}, u32[]{:S(2)}) collective-permute-start(f32[512,128]{1,0:T(8,128)S(1)} %shard_map.67), channel_id=1, source_target_pairs={{0,2},{1,3},{2,0},{3,1},{4,6},{5,7},{6,4},{7,5},{8,10},{9,11},{10,... | collective-permute-start | bytes 786440 | tf_op jit(solution)/shard_map/ppermute | solution.py:499
where the time goes:
time: 107 us; the launch traced here: 106 us
  Pallas kernels  58.3 us (54%)
  waiting for transfers between devices  27.1 us (25%)
  starting transfers between devices  19.2 us (18%)
  local copies, waits for them, and re-layouts  1.46 us (1%)
    ppermute x4, waiting for transfers between devices, body(): siblings.append(lax.ppermute(current, axis, pairs))  22.1 us
    pallas_call x4, Pallas kernels, own(): pl.pallas_call(functools.partial(own_kernel, unit, tiles, chunk), in_spec...  21.1 us
    pallas_call x1, Pallas kernels, body(): pl.pallas_call(functools.partial(final_kernel, unit, levels), in_specs=[v...  15.5 us
    ppermute x4, starting transfers between devices, body(): siblings.append(lax.ppermute(current, axis, pairs))  13.7 us
    pallas_call x1, Pallas kernels, body(): pl.pallas_call(functools.partial(cross_kernel, unit), grid=(2,), in_specs...  9.09 us
    pallas_call x1, Pallas kernels, body(): pl.pallas_call(functools.partial(places_kernel, unit), grid=(points // GR...  5.09 us
    pallas_call x1, Pallas kernels, body(): pl.pallas_call(functools.partial(core_kernel, unit), in_specs=[vmem] * 6,...  5.09 us
    ppermute x1, waiting for transfers between devices, body(): relay = lax.ppermute(lower, 'leaf', to_relay)  3.57 us
  transfers between devices with their start and end apart: 8, of which 6 were waited for; matrix products, arithmetic and copies ran while one was open for 0% of the time, Pallas kernels for 22%

commit v1 on v0

--- a/solution.py
+++ b/solution.py
@@ -37,6 +37,11 @@
     return high, (value - high.astype(F32)).astype(BF16)
 
 
+def remainders(value, high):
+    rest = (value - high.astype(F32)).astype(BF16)
+    return (rest * BF16(LO_UP)).astype(WIDE8), (high * BF16(FULL_UP)).astype(WIDE8)
+
+
 def strip_indices(order_ref, tail, width):
     count = order_ref.shape[1]
     return jnp.where(tail, order_ref[:, count - width :], order_ref[:, :width])
@@ -73,35 +78,55 @@
         fine_ref[pl.ds(first, ROWS), :] = hit.astype(FINE8)
 
 
-def cross_kernel(unit, order_ref, jitter_ref, x_ref, upper_ref, lower_ref, high_ref, low_ref, sel_ref, sel8_ref):
-    step = pl.program_id(0)
-    points = high_ref.shape[1]
+def cross_kernel(unit, order_ref, jitter_ref, x_ref, upper_ref, lower_ref, high_ref, low_ref, sel_ref, sel8_ref, x_buf, sems):
+    count, points = high_ref.shape
     width = upper_ref.shape[1]
-    rows = high_ref.shape[0]
+    pieces = points // LANES
+    parts = x_buf.shape[0]
+    rows = count // parts
     tail = (lax.axis_index("leaf") & 1) == 1
 
-    @pl.when(step == 0)
-    def _():
-        fill_selector(strip_indices(order_ref, tail, width), sel_ref, sel8_ref)
-        upper_ref[rows:, :] = stack_rows(strip_places(jitter_ref, tail, width, unit), 8)
-
-    pieces = points // LANES
-    for piece in range(pieces):
-        value = x_ref[pl.ds(piece, rows, stride=pieces), :]
-        high = value.astype(BF16)
-        lanes = pl.ds(piece * LANES, LANES)
-        high_ref[:, lanes] = high
-        low_ref[:, lanes] = ((value - high.astype(F32)) * LO_UP).astype(WIDE8)
-        low_ref[:, pl.ds(points + piece * LANES, LANES)] = (value * FULL_UP).astype(WIDE8)
-    picked = dot(high_ref[...], sel_ref[...]) + dot(low_ref[:, :points], sel8_ref[...]) * (1.0 / LO_UP)
-
-    @pl.when(step == 0)
-    def _():
-        upper_ref[:rows, :] = picked
-
-    @pl.when(step == 1)
-    def _():
-        lower_ref[...] = picked
+    def copies(part):
+        here = pl.ds(part * rows, rows)
+        return [
+            pltpu.make_async_copy(x_ref.at[here, piece, :], x_buf.at[part, piece], sems.at[part, piece])
+            for piece in range(pieces)
+        ]
+
+    def split(part):
+        here = pl.ds(pl.multiple_of(part * rows, rows), rows)
+        for piece in range(pieces):
+            value = x_buf[part, piece]
+            high = value.astype(BF16)
+            lanes = pl.ds(piece * LANES, LANES)
+            high_ref[here, lanes] = high
+            low_ref[here, lanes], low_ref[here, pl.ds(points + piece * LANES, LANES)] = remainders(value, high)
+
+    def pick(first, size):
+        here = pl.ds(first, size)
+        return dot(high_ref[here, :], sel_ref[...]) + dot(low_ref[here, :points], sel8_ref[...]) * (1.0 / LO_UP)
+
+    for part in range(parts):
+        for copy in copies(part):
+            copy.start()
+    half = count // 2
+    fill_selector(strip_indices(order_ref, tail, width), sel_ref, sel8_ref)
+    upper_ref[half:, :] = stack_rows(strip_places(jitter_ref, tail, width, unit), 8)
+
+    def early(part, carry):
+        for copy in copies(part):
+            copy.wait()
+        split(part)
+        return carry
+
+    lax.fori_loop(0, parts // 2, early, 0)
+    for part in range(parts // 2, parts):
+        for copy in copies(part):
+            copy.wait()
+    for part in range(parts // 2, parts):
+        split(part)
+    upper_ref[:half, :] = pick(0, half)
+    lower_ref[...] = pick(half, half)
 
 
 def places_kernel(unit, order_ref, jitter_ref, base_ref, spread_ref, base16_ref, base8_ref, far_ref, packed_ref):
@@ -153,12 +178,13 @@
     return jnp.concatenate([jnp.where(left, wide, 0.0), jnp.where(left, 0.0, wide)], axis=0)
 
 
-def matrices_kernel(leaf_levels, transfer_ref, coupling_ref, lift_ref, couple_ref):
+def matrices_kernel(leaf_levels, transfer_ref, coupling_ref, lift_ref, couple_ref, last_ref):
     levels = transfer_ref.shape[0]
     leaf = lax.axis_index("leaf")
     sub = lax.axis_index("sub")
     down = None
     span = 2 * transfer_ref.shape[2]
+    upper = levels - 1
     for level in range(levels):
         bit = leaf >> level & 1 if level < leaf_levels else sub >> (level - leaf_levels) & 1
         right = bit == 1
@@ -169,11 +195,17 @@
         if down is not None:
             couple = jnp.dot(couple, down, precision=PRECISE, preferred_element_type=F32)
         high, low = split2(twice(couple))
-        couple_ref[pl.ds(level * span, span), :] = high
-        couple_ref[pl.ds((levels + level) * span, span), :] = high
-        couple_ref[pl.ds((2 * levels + level) * span, span), :] = low
+        if level == 0:
+            step_high, step_low = split2(twice(own.T))
+            for position, part in enumerate((high, step_high, high, step_high, low, step_low)):
+                last_ref[pl.ds(position * span, span), :] = part
+        else:
+            couple_ref[pl.ds((level - 1) * span, span), :] = high
+            couple_ref[pl.ds((upper + level - 1) * span, span), :] = high
+            couple_ref[pl.ds((2 * upper + level - 1) * span, span), :] = low
         if level < levels - 1:
-            down = own.T if down is None else jnp.dot(own.T, down, precision=PRECISE, preferred_element_type=F32)
+            if level > 0:
+                down = own.T if down is None else jnp.dot(own.T, down, precision=PRECISE, preferred_element_type=F32)
             own_high, own_low = split2(twice(own))
             other_high, other_low = split2(twice(other))
             for position, part in enumerate((own_high, other_high, own_high, other_high, own_low, other_low)):
@@ -200,11 +232,26 @@
     strip_ref[:count, :width] = dot(high, sel_ref[...]) + dot(low, sel8_ref[...]) * (1.0 / LO_UP)
 
 
-def lift_kernel(own_ref, other_ref, matrix_ref, out_ref):
-    own_high, own_low = split2(own_ref[...])
-    other_high, other_low = split2(other_ref[...])
-    stacked = jnp.concatenate([own_high, other_high, own_low, other_low, own_high, other_high], axis=1)
-    out_ref[...] = dot(stacked, matrix_ref[0])
+def split_product(values, matrix):
+    parts = [split2(value) for value in values]
+    stacked = [p[0] for p in parts] + [p[1] for p in parts] + [p[0] for p in parts]
+    return dot(jnp.concatenate(stacked, axis=1), matrix)
+
+
+def lift_kernel(level, own_ref, other_ref, matrix_ref, out_ref):
+    out_ref[...] = split_product([own_ref[...], other_ref[...]], matrix_ref[level])
+
+
+def first_lift_kernel(own_ref, other_ref, matrix_ref, out_ref):
+    rows = out_ref.shape[0]
+    width = own_ref.shape[1] - LANES
+    here = pl.ds(pl.multiple_of((lax.axis_index("leaf") & 1) * rows, rows), rows)
+    out_ref[...] = split_product([own_ref[here, width:], other_ref[here, width:]], matrix_ref[0])
+
+
+def collect_kernel(*refs):
+    sib_refs, couple_ref, out_ref = refs[:-2], refs[-2], refs[-1]
+    out_ref[...] = split_product([ref[...] for ref in sib_refs], couple_ref[...])
 
 
 def target_places(jitter_ref, unit, place_ref):
@@ -214,9 +261,10 @@
     place_ref[...] = stack_rows(rows, 8)
 
 
-def fill_weights(unit, place_ref, spread_ref, high_ref, fine_ref, columns, sources):
+def fill_weights(unit, place_ref, spread_ref, high_ref, fine_ref, columns, sources, looped=False):
     root = unit * math.sqrt(DELTA_SQ)
-    for block in range(0, sources, ROWS):
+
+    def one(block):
         here = pl.ds(block, ROWS)
         for part in range(TILE // LANES):
             lanes = pl.ds(part * LANES, LANES)
@@ -227,77 +275,116 @@
                 square = gap * gap + square
             store_weight(square, high_ref, fine_ref, here, pl.ds(sources + block, ROWS), lanes)
 
-
-def own_kernel(unit, tiles, chunk, jitter_ref, spread_ref, high_ref, low_ref, *refs):
-    out_ref, place_ref, ha, wa, hb, wb = refs[-6:]
+    if looped:
+
+        def run(index, carry):
+            one(pl.multiple_of(index * ROWS, ROWS))
+            return carry
+
+        lax.fori_loop(0, sources // ROWS, run, 0)
+    else:
+        for block in range(0, sources, ROWS):
+            one(block)
+
+
+def own_kernel(unit, chunk, jitter_ref, spread_ref, high_ref, low_ref, *refs):
+    out_ref, ha, wa, place_ref, hb, wb = refs[-6:]
+    chunks = out_ref.shape[0]
     points = high_ref.shape[1]
     target_places(jitter_ref, unit, place_ref)
-    buffers = ((ha, wa), (hb, wb))
-
-    def fill(tile):
-        high, fine = buffers[tile % 2]
-        fill_weights(unit, place_ref, spread_ref, high, fine, (chunk * tiles + tile) * TILE, points)
-
-    fill(0)
-    for tile in range(tiles):
-        if tile + 1 < tiles:
-            fill(tile + 1)
-        high, fine = buffers[tile % 2]
-        out_ref[chunk, :, tile * TILE : (tile + 1) * TILE] = (
-            dot(high_ref[...], high[...]) + dot(low_ref[...], fine[...]) * NEAR_DOWN
-        )
+
+    def fill(tile, high, fine, looped=False):
+        fill_weights(unit, place_ref, spread_ref, high, fine, tile * TILE, points, looped)
+
+    def product(tile, high, fine):
+        value = dot(high_ref[...], high[...]) + dot(low_ref[...], fine[...]) * NEAR_DOWN
+        out_ref[chunk, :, tile * TILE : (tile + 1) * TILE] = value
+
+    if chunk == 0:
+        fill(0, ha, wa, True)
+    fill(2 * chunk + 1, hb, wb)
+    product(0, ha, wa)
+    if chunk + 1 < chunks:
+        fill(2 * chunk + 2, ha, wa)
+    product(1, hb, wb)
 
 
 def store_weight(square, high_ref, fine_ref, here, there, lanes):
     weight = lax.rsqrt(square)
     high = weight.astype(BF16)
     high_ref[here, lanes] = high
-    fine_ref[here, lanes] = (weight * W_UP).astype(FINE8)
-    fine_ref[there, lanes] = ((weight - high.astype(F32)) * W_LO_UP).astype(FINE8)
-
-
-def final_kernel(unit, levels, *refs):
-    jitter_ref, core_ref, upper_ref, lower_ref = refs[:4]
-    sib_refs = refs[4 : 4 + levels]
-    couple_ref, far_ref = refs[4 + levels : 6 + levels]
-    near_ref, out_ref, left_ref, low_ref, spread_ref, place_ref, ha, wa, hb, wb, stage_ref, sems = refs[6 + levels :]
+    fine_ref[here, lanes] = (high * BF16(W_UP)).astype(FINE8)
+    rest = (weight - high.astype(F32)).astype(BF16)
+    fine_ref[there, lanes] = (rest * BF16(W_LO_UP)).astype(FINE8)
+
+
+def place_strip(spread_ref, across, shift):
+    for component in range(3):
+        column = across[:, component : component + 1]
+        if component == 0:
+            column = column + shift
+        spread_ref[component] = jnp.broadcast_to(column, spread_ref.shape[1:])
+
+
+def take_strip(left_ref, low_ref, rows, value):
+    width = value.shape[1]
+    high = value.astype(BF16)
+    left_ref[rows, :width] = high
+    low_ref[rows, :width], low_ref[rows, width:] = remainders(value, high)
+
+
+def core_shift(unit):
+    odd = (lax.axis_index("leaf") & 1) == 1
+    return jnp.where(odd, -unit, unit)
+
+
+def middle_kernel(unit, jitter_ref, core_ref, near_ref, out_ref, left_ref, low_ref, spread_ref, place_ref, ha, wa, hb, wb):
+    chunks, count, _ = near_ref.shape
+    width = left_ref.shape[1]
+    target_places(jitter_ref, unit, place_ref)
+    place_strip(spread_ref, core_ref[count:, :width].T, core_shift(unit))
+
+    def fill(tile, high, fine):
+        fill_weights(unit, place_ref, spread_ref, high, fine, pl.multiple_of(tile * TILE, TILE), width)
+
+    fill_weights(unit, place_ref, spread_ref, ha, wa, 0, width, True)
+    take_strip(left_ref, low_ref, pl.ds(0, count), core_ref[:count, :width])
+
+    def product(pair, tile, h, w):
+        lanes = slice(tile * TILE, (tile + 1) * TILE)
+        out_ref[pair, :, lanes] = (
+            near_ref[pair, :, lanes] + dot(left_ref[...], h[...]) + dot(low_ref[...], w[...]) * NEAR_DOWN
+        )
+
+    def run(pair, carry):
+        fill(2 * pair + 1, hb, wb)
+        product(pair, 0, ha, wa)
+        fill(jnp.minimum(2 * pair + 2, 2 * chunks - 1), ha, wa)
+        product(pair, 1, hb, wb)
+        return carry
+
+    lax.fori_loop(0, chunks, run, 0)
+
+
+def final_kernel(unit, jitter_ref, core_ref, upper_ref, lower_ref, mine_ref, other_ref, last_ref, far_ref, near_ref, *refs):
+    out_ref, left_ref, low_ref, spread_ref, place_ref, ha, wa, hb, wb, stage_ref, sems = refs
     chunks, count, _ = near_ref.shape
     width = upper_ref.shape[1]
-    sources = 2 * width
 
     def fill(tile, high, fine):
         columns = pl.multiple_of(tile * TILE, TILE)
-        fill_weights(unit, place_ref, spread_ref, high, fine, columns, sources)
-        high[sources:, :] = far_ref[:, pl.ds(columns, TILE)]
+        fill_weights(unit, place_ref, spread_ref, high, fine, columns, width)
+        high[width:, :] = far_ref[:, pl.ds(columns, TILE)]
 
     target_places(jitter_ref, unit, place_ref)
-    odd = (lax.axis_index("leaf") & 1) == 1
-    sign = jnp.where(odd, unit, -unit)
-
-    def place_strip(position, across, shift):
-        lanes = pl.ds(position * width, width)
-        for component in range(3):
-            column = across[:, component : component + 1]
-            if component == 0:
-                column = column + shift
-            spread_ref[component, lanes, :] = jnp.broadcast_to(column, (width, LANES))
-
-    def take_strip(position, rows, value):
-        high = value.astype(BF16)
-        lanes = pl.ds(position * width, width)
-        left_ref[rows, lanes] = high
-        low_ref[rows, lanes] = ((value - high.astype(F32)) * LO_UP).astype(WIDE8)
-        low_ref[rows, pl.ds(sources + position * width, width)] = (value * FULL_UP).astype(WIDE8)
-
-    place_strip(0, core_ref[count:, :width].T, -sign)
-    place_strip(1, upper_ref[count // 2 :, :].T, sign)
+    place_strip(spread_ref, upper_ref[count // 2 :, :].T, -core_shift(unit))
     fill(0, ha, wa)
-    take_strip(0, pl.ds(0, count), core_ref[:count, :width])
-    take_strip(1, pl.ds(0, count // 2), upper_ref[: count // 2, :])
-    take_strip(1, pl.ds(count // 2, count // 2), lower_ref[...])
-    parts = [split2(sib_refs[0][: count // 2, width:])] + [split2(ref[...]) for ref in sib_refs[1:]]
-    stacked = jnp.concatenate([p[0] for p in parts] + [p[1] for p in parts] + [p[0] for p in parts], axis=1)
-    expansion = dot(stacked, couple_ref[...])
+    take_strip(left_ref.at[:, pl.ds(0, width)], low_ref, pl.ds(0, count // 2), upper_ref[: count // 2, :])
+    take_strip(left_ref.at[:, pl.ds(0, width)], low_ref, pl.ds(count // 2, count // 2), lower_ref[...])
+    even = (lax.axis_index("leaf") & 1) == 0
+    mine, other = mine_ref[...], other_ref[...]
+    above = jnp.concatenate([jnp.where(even, mine, other), jnp.where(even, other, mine)], axis=0)
+    expansion = split_product([core_ref[: count // 2, width:], above], last_ref[...])
     high = expansion.astype(BF16).astype(F32)
     low = pltpu.roll(expansion - high, LANES // 2, 1)
     half = GROUP // 2
@@ -305,12 +392,12 @@
     for block in range(count // GROUP):
         h = high[block * half : (block + 1) * half]
         l = low[block * half : (block + 1) * half]
-        upper = pl.ds(block * GROUP, half)
-        lower = pl.ds(block * GROUP + half, half)
-        left_ref[upper, sources : sources + LANES] = jnp.where(is_left, h, l).astype(BF16)
-        left_ref[lower, sources : sources + LANES] = jnp.where(is_left, l, h).astype(BF16)
-        left_ref[upper, sources + LANES :] = jnp.where(is_left, h, 0.0).astype(BF16)
-        left_ref[lower, sources + LANES :] = jnp.where(is_left, 0.0, h).astype(BF16)
+        first = pl.ds(block * GROUP, half)
+        second = pl.ds(block * GROUP + half, half)
+        left_ref[first, width : width + LANES] = jnp.where(is_left, h, l).astype(BF16)
+        left_ref[second, width : width + LANES] = jnp.where(is_left, l, h).astype(BF16)
+        left_ref[first, width + LANES :] = jnp.where(is_left, h, 0.0).astype(BF16)
+        left_ref[second, width + LANES :] = jnp.where(is_left, 0.0, h).astype(BF16)
 
     parts_per_tile = TILE // LANES
 
@@ -375,34 +462,35 @@
     levels = leaf_levels + sub_levels
     half = count // 2
     pieces = points // LANES
-    x = charges.reshape(count * pieces, LANES)
+    x = charges.reshape(count, pieces, LANES)
     order = ordering.reshape(1, points)
     offsets = jitter.reshape(3, 1, points)
     base = leaf_bases.reshape(rank, points)
     params = lambda mib: pltpu.CompilerParams(vmem_limit_bytes=mib << 20)
     vmem = pl.BlockSpec(memory_space=pltpu.VMEM)
 
+    in_hbm = lambda array: pltpu.with_memory_space_constraint(array, pltpu.HBM)
+    parts = 4
     upper, lower, high, low = pl.pallas_call(
         functools.partial(cross_kernel, unit),
-        grid=(2,),
-        in_specs=[whole(order), whole(offsets), pl.BlockSpec((half * pieces, LANES), lambda i: (i, 0))],
-        out_specs=[
-            pl.BlockSpec((half + 8, width), lambda i: (0, 0)),
-            pl.BlockSpec((half, width), lambda i: (0, 0)),
-            pl.BlockSpec((half, points), lambda i: (i, 0)),
-            pl.BlockSpec((half, 2 * points), lambda i: (i, 0)),
-        ],
+        in_specs=[vmem, vmem, pl.BlockSpec(memory_space=pltpu.HBM)],
+        out_specs=[vmem] * 4,
         out_shape=[
             shape((half + 8, width)),
             shape((half, width)),
             shape((count, points), BF16),
             shape((count, 2 * points), WIDE8),
         ],
-        scratch_shapes=[pltpu.VMEM((points, width), BF16), pltpu.VMEM((points, width), FINE8)],
-        compiler_params=params(30),
+        scratch_shapes=[
+            pltpu.VMEM((points, width), BF16),
+            pltpu.VMEM((points, width), FINE8),
+            pltpu.VMEM((parts, pieces, count // parts, LANES), F32),
+            pltpu.SemaphoreType.DMA((parts, pieces)),
+        ],
+        compiler_params=params(20),
         cost_estimate=cost(3 * count * points * width, 16 * count * points),
         name="cross",
-    )(order, offsets, pltpu.with_memory_space_constraint(x, pltpu.HBM))
+    )(order, offsets, in_hbm(x))
     last = leaf_count - 1
     middle = leaf_count // 2
     up_pairs = [(i, i + 1) for i in range(1, last, 2)]
@@ -449,79 +537,101 @@
     )(order, offsets, base16, base8, high, low)
     core_in = lax.ppermute(core, "leaf", [(i, i ^ 1) for i in range(leaf_count)])
 
-    lift, couple = pl.pallas_call(
+    lift, couple, last_matrix = pl.pallas_call(
         functools.partial(matrices_kernel, leaf_levels),
         in_specs=[vmem] * 2,
-        out_specs=[vmem] * 2,
-        out_shape=[shape((levels - 1, 12 * rank, 2 * rank), BF16), shape((6 * levels * rank, 2 * rank), BF16)],
+        out_specs=[vmem] * 3,
+        out_shape=[
+            shape((levels - 1, 12 * rank, 2 * rank), BF16),
+            shape((6 * (levels - 1) * rank, 2 * rank), BF16),
+            shape((12 * rank, 2 * rank), BF16),
+        ],
         compiler_params=params(8),
         cost_estimate=cost(1e6, 1e6),
         name="matrices",
     )(transfer, coupling)
 
-    tiles = 2
-    chunks = points // (tiles * TILE)
-    near = None
-
-    def own(chunk, near):
-        operands = (offsets, spread, high, low) + (() if near is None else (near,))
+    chunks = points // (2 * TILE)
+
+    def own(chunk, *carried):
         return pl.pallas_call(
-            functools.partial(own_kernel, unit, tiles, chunk),
-            in_specs=[vmem] * 4 + ([] if near is None else [pl.BlockSpec(memory_space=pl.ANY)]),
+            functools.partial(own_kernel, unit, chunk),
+            in_specs=[vmem] * 4 + [pl.BlockSpec(memory_space=pl.ANY)] * len(carried),
+            out_specs=[vmem] * 3,
+            out_shape=[shape((chunks, count, 2 * TILE)), shape((points, TILE), BF16), shape((2 * points, TILE), FINE8)],
+            scratch_shapes=[
+                pltpu.VMEM((8, points), F32),
+                pltpu.VMEM((points, TILE), BF16),
+                pltpu.VMEM((2 * points, TILE), FINE8),
+            ],
+            input_output_aliases={4 + i: i for i in range(len(carried))},
+            compiler_params=params(8),
+            cost_estimate=cost(8 * count * points * TILE, 10 * count * points),
+        )(offsets, spread, high, low, *carried)
+
+    quarter = half // 2
+
+    def small(kernel, operands):
+        return pl.pallas_call(
+            kernel,
+            in_specs=[vmem] * len(operands),
             out_specs=vmem,
-            out_shape=shape((chunks, count, tiles * TILE)),
-            scratch_shapes=[pltpu.VMEM((8, points), F32)]
-            + [pltpu.VMEM((points, TILE), BF16), pltpu.VMEM((2 * points, TILE), FINE8)] * 2,
-            input_output_aliases={} if near is None else {4: 0},
-            compiler_params=params(12),
-            cost_estimate=cost(4 * count * points * tiles * TILE, 10 * count * points),
+            out_shape=shape((quarter, LANES)),
+            compiler_params=params(4),
+            cost_estimate=cost(2 * quarter * 768 * 128, 3 * quarter * 512),
         )(*operands)
 
-    def lifted(level, own_moment, other, from_strip):
-        spec = pl.BlockSpec((half, LANES), (lambda i: (0, width // LANES)) if from_strip else (lambda i: (0, 0)))
-        return pl.pallas_call(
-            lift_kernel,
-            grid=(1,),
-            in_specs=[spec, spec, pl.BlockSpec((1, 12 * rank, 2 * rank), lambda i: (level, 0, 0))],
-            out_specs=pl.BlockSpec((half, LANES), lambda i: (0, 0)),
-            out_shape=shape((half, LANES)),
-            compiler_params=params(8),
-            cost_estimate=cost(2 * half * 768 * 128, 3 * half * 512),
-        )(own_moment, other, lift)
-
-    near = own(0, None)
-    siblings = [core_in]
-    current = core
+    carried = own(0)
+    siblings = []
+    current = small(first_lift_kernel, (core, core_in, lift))
     for level in range(1, levels):
-        current = lifted(level - 1, current, siblings[-1], level == 1)
+        if level > 1:
+            kernel = functools.partial(lift_kernel, level - 1)
+            current = small(kernel, (current, siblings[-1], lift))
         axis, bit = ("leaf", level) if level < leaf_levels else ("sub", level - leaf_levels)
         pairs = [(i, i ^ 1 << bit) for i in range(lax.axis_size(axis))]
         siblings.append(lax.ppermute(current, axis, pairs))
         if level == 1:
             lower_in = lax.ppermute(relay, "leaf", relayed)
         if level < chunks:
-            near = own(level, near)
+            carried = own(level, *carried)
     for chunk in range(levels, chunks):
-        near = own(chunk, near)
-
-    sources = 2 * width
+        carried = own(chunk, *carried)
+    mine = small(collect_kernel, (*siblings, couple))
+    other = lax.ppermute(mine, "leaf", [(i, i ^ 1) for i in range(leaf_count)])
+
+    def strip_scratch(extra):
+        tall = width + extra
+        return [
+            pltpu.VMEM((count, tall), BF16),
+            pltpu.VMEM((count, 2 * width), WIDE8),
+            pltpu.VMEM((3, width, LANES), F32),
+            pltpu.VMEM((8, points), F32),
+        ] + [pltpu.VMEM((tall, TILE), BF16), pltpu.VMEM((2 * width, TILE), FINE8)] * 2
+
+    near = pl.pallas_call(
+        functools.partial(middle_kernel, unit),
+        in_specs=[vmem] * 3,
+        out_specs=vmem,
+        out_shape=shape((chunks, count, 2 * TILE)),
+        scratch_shapes=strip_scratch(0),
+        input_output_aliases={2: 0},
+        compiler_params=params(12),
+        cost_estimate=cost(4 * count * points * width, 8 * count * points),
+        name="middle",
+    )(offsets, core_in, carried[0])
+
     out = pl.pallas_call(
-        functools.partial(final_kernel, unit, levels),
-        in_specs=[vmem] * (7 + levels),
+        functools.partial(final_kernel, unit),
+        in_specs=[vmem] * 9,
         out_specs=pl.BlockSpec(memory_space=pl.ANY),
         out_shape=shape((count, pieces, LANES)),
-        scratch_shapes=[
-            pltpu.VMEM((count, sources + 4 * rank), BF16),
-            pltpu.VMEM((count, 2 * sources), WIDE8),
-            pltpu.VMEM((3, sources, LANES), F32),
-            pltpu.VMEM((8, points), F32),
-        ]
-        + [pltpu.VMEM((sources + 4 * rank, TILE), BF16), pltpu.VMEM((2 * sources, TILE), FINE8)] * 2
+        scratch_shapes=strip_scratch(4 * rank)
         + [pltpu.VMEM((4, count * TILE // LANES, LANES), F32), pltpu.SemaphoreType.DMA((4,))],
-        compiler_params=params(24),
-        cost_estimate=cost(4 * count * points * sources, 8 * count * points),
+        compiler_params=params(20),
+        cost_estimate=cost(4 * count * points * width, 8 * count * points),
         name="final",
-    )(offsets, core_in, upper_in, lower_in, *siblings, couple, far, near)
+    )(offsets, core_in, upper_in, lower_in, mine, other, last_matrix, far, near)
     return out.reshape(charges.shape)
 
 

time: 107 us -> 95.9 us (0.90)
  waiting for transfers between devices: 27.1 us -> 19.6 us
  starting transfers between devices: 19.2 us -> 15 us
    ppermute x4, waiting for transfers between devices: 22.1 us -> 18 us  [body(): siblings.append(lax.ppermute(current, axis, pairs))]
    ppermute x4, starting transfers between devices: 13.7 us -> 10.1 us  [body(): siblings.append(lax.ppermute(current, axis, pairs))]
    ppermute x1, waiting for transfers between devices: 3.57 us -> 0.01 us  [body(): relay = lax.ppermute(lower, 'leaf', to_relay)]
    ppermute x1, starting transfers between devices: 2.74 us -> 1.58 us  [body(): lower_in = lax.ppermute(relay, 'leaf', relayed)]
    pallas_call x10 -> x12, Pallas kernels: 47.2 us -> 48.1 us  [the longest x4 21.5 us: own(): pl.pallas_call(functools.partial(own_kernel, unit, chunk), in_specs=[vmem...]
  transfers between devices with their start and end apart: 8 -> 9, of which waited for: 6 -> 3; matrix products, arithmetic and copies ran while one was open for 0% -> 0% of each run, Pallas kernels for 22% -> 32%
where the time goes in v1:
time: 95.9 us; the launch traced here: 95.6 us
  Pallas kernels  59.1 us (62%)
  waiting for transfers between devices  19.6 us (20%)
  starting transfers between devices  15 us (16%)
  local copies, waits for them, and re-layouts  1.46 us (2%)
    pallas_call x4, Pallas kernels, own(): pl.pallas_call(functools.partial(own_kernel, unit, chunk), in_specs=[vmem...  21.5 us
    ppermute x4, waiting for transfers between devices, body(): siblings.append(lax.ppermute(current, axis, pairs))  18 us
    ppermute x4, starting transfers between devices, body(): siblings.append(lax.ppermute(current, axis, pairs))  10.1 us
    pallas_call x1, Pallas kernels, body(): pl.pallas_call(functools.partial(final_kernel, unit), in_specs=[vmem] * 9...  9.27 us
    pallas_call x1, Pallas kernels, body(): pl.pallas_call(functools.partial(cross_kernel, unit), in_specs=[vmem, vme...  8.69 us
    pallas_call x1, Pallas kernels, body(): pl.pallas_call(functools.partial(middle_kernel, unit), in_specs=[vmem] *...  7.36 us
    pallas_call x1, Pallas kernels, body(): pl.pallas_call(functools.partial(places_kernel, unit), grid=(points // GR...  5.1 us
    pallas_call x1, Pallas kernels, body(): pl.pallas_call(functools.partial(core_kernel, unit), in_specs=[vmem] * 6,...  5.1 us
  transfers between devices with their start and end apart: 9, of which 3 were waited for; matrix products, arithmetic and copies ran while one was open for 0% of the time, Pallas kernels for 32%

profile of v1, /device:TPU:0, one launch (start us, length us, event | category | flops | bytes accessed | tf_op | source)
XLA Modules:
  0.0 95.6 jit_solution(15287880545472337321)
XLA Ops:
  0.0 0.7 copy-done
  0.7 0.7 copy-done.5
  1.4 8.7 %cross.1 = (f32[520,512]{1,0:T(8,128)S(1)}, f32[512,512]{1,0:T(8,128)S(1)}, bf16[1024,2048]{1,0:T(8,128)(2,1)S(1)}, f8e5m2[1024,4096]{1,0:T(32,128)(4,1)S(1)}) custom-call(s32[1,2048]{1,0:T(1,128)S(1)} %bitcast.15, f32[3,1,2048]{2,1,0:T(1,128)S(1)} %bitcast.5, f32[1024,16,128]{2,1,0:T(8,128)} %bitcast.18), custom_call_target="tpu_custom_call" | custom-call | flops 3221225472 | bytes 33554432 | tf_op jit(solution)/shard_map/cross/pallas_call | solution.py:474
  10.2 5.1 %places.1 = (f32[3,2048,128]{2,1,0:T(8,128)S(1)}, bf16[2048,256]{1,0:T(8,128)(2,1)S(1)}, f8e4m3fn[2048,128]{1,0:T(32,128)(4,1)S(1)}, bf16[256,2048]{1,0:T(8,128)(2,1)S(1)}) custom-call(s32[1,2048]{1,0:T(1,128)S(1)} %bitcast.16, f32[3,1,2048]{2,1,0:T(1,128)S(1)} %bitcast.6, f32[64,2048]{1,0:T(8,128)S(1)} %bitcast.14), custom_call_target="tpu_custom_call" | custom-call | flops 2147483648 | bytes 10485760 | tf_op jit(solution)/shard_map/places/pallas_call | solution.py:506
  15.3 0.0 copy-start.2
  15.3 0.0 copy-start.3
  15.3 5.1 %core.1.own_ref = f32[1032,640]{1,0:T(8,128)S(1)} custom-call(s32[1,2048]{1,0:T(1,128)S(1)} %bitcast.17, f32[3,1,2048]{2,1,0:T(1,128)S(1)} %bitcast.7, bf16[2048,256]{1,0:T(8,128)(2,1)S(1)} %get-tuple-element.26.base16_ref, f8e4m3fn[2048,128]{1,0:T(32,128)(4,1)S(1)} %get-tuple-element.27.base8_ref, bf16[1024,2048]{1,0:T(8,128)(2,1)S(1)} %get-tuple-element.28.high_ref, ...), custom_call_target="tpu_custom_call" | custom-call | flops 4831838208 | bytes 12582912 | tf_op jit(solution)/shard_map/core/pallas_call | solution.py:528
  20.4 0.5 collective-permute-start
  21.0 1.3 %collective-permute-start.2 = (f32[512,512]{1,0:T(8,128)S(1)}, f32[512,512]{1,0:T(8,128)S(1)}, u32[]{:S(2)}, u32[]{:S(2)}) collective-permute-start(f32[512,512]{1,0:T(8,128)S(1)} %get-tuple-element.31), channel_id=1, source_target_pairs={{12,28},{16,0},{4,4},{8,8},{20,20},{24,24},{13,29},{17,1},{5,5},{9... | collective-permute-start | bytes 3145736 | tf_op jit(solution)/shard_map/ppermute | solution.py:504
  22.2 0.9 collective-permute-start.1
  23.2 0.8 matrices.1
  23.9 1.6 %collective-permute-done.other_ref.core_ref = f32[1032,640]{1,0:T(8,128)S(1)} collective-permute-done((f32[1032,640]{1,0:T(8,128)S(1)}, f32[1032,640]{1,0:T(8,128)S(1)}, u32[]{:S(2)}, u32[]{:S(2)}) %collective-permute-start) | collective-permute-done | bytes 2641952 | tf_op jit(solution)/shard_map/ppermute | solution.py:538
  25.5 0.2 shard_map.64.own_ref
  25.8 2.9 %collective-permute-start.4 = (f32[256,128]{1,0:T(8,128)S(1)}, f32[256,128]{1,0:T(8,128)S(1)}, u32[]{:S(2)}, u32[]{:S(2)}) collective-permute-start(f32[256,128]{1,0:T(8,128)S(1)} %shard_map.64.own_ref), channel_id=1, source_target_pairs={{0,8},{4,12},{8,0},{12,4},{16,24},{20,28},{24,16},{28,20},{1,9},{5... | collective-permute-start | bytes 393224 | tf_op jit(solution)/shard_map/ppermute | solution.py:593
  28.7 6.3 %shard_map.69 = (f32[4,1024,512]{2,1,0:T(8,128)S(1)}, bf16[2048,256]{1,0:T(8,128)(2,1)S(1)}, f8e4m3fn[4096,256]{1,0:T(32,128)(4,1)S(1)}) custom-call(f32[3,1,2048]{2,1,0:T(1,128)S(1)} %bitcast.8, f32[3,2048,128]{2,1,0:T(8,128)S(1)} %get-tuple-element.36.spread_ref, bf16[1024,2048]{1,0:T(8,128)(2,1)S(1)} %get-tuple-element.28.high_ref, ...), custom_call_target="tpu_custom_call" | custom-call | flops 4294967296 | bytes 20971520 | tf_op jit(solution)/shard_map/pallas_call | solution.py:557
  35.0 16.0 %collective-permute-done.4.other_ref.refs_0_ = f32[256,128]{1,0:T(8,128)S(1)} collective-permute-done((f32[256,128]{1,0:T(8,128)S(1)}, f32[256,128]{1,0:T(8,128)S(1)}, u32[]{:S(2)}, u32[]{:S(2)}) %collective-permute-start.4) | collective-permute-done | bytes 131104 | tf_op jit(solution)/shard_map/ppermute | solution.py:593
  51.0 0.3 shard_map.65.own_ref
  51.3 2.8 %collective-permute-start.5 = (f32[256,128]{1,0:T(8,128)S(1)}, f32[256,128]{1,0:T(8,128)S(1)}, u32[]{:S(2)}, u32[]{:S(2)}) collective-permute-start(f32[256,128]{1,0:T(8,128)S(1)} %shard_map.65.own_ref), channel_id=1, source_target_pairs={{0,16},{4,20},{8,24},{12,28},{16,0},{20,4},{24,8},{28,12},{1,17},{... | collective-permute-start | bytes 393224 | tf_op jit(solution)/shard_map/ppermute | solution.py:593
  54.1 5.1 %shard_map.70 = (f32[4,1024,512]{2,1,0:T(8,128)S(1)}, bf16[2048,256]{1,0:T(8,128)(2,1)S(1)}, f8e4m3fn[4096,256]{1,0:T(32,128)(4,1)S(1)}) custom-call(f32[3,1,2048]{2,1,0:T(1,128)S(1)} %bitcast.9, f32[3,2048,128]{2,1,0:T(8,128)S(1)} %get-tuple-element.36.spread_ref, ...), custom_call_target="tpu_custom_call", output_to_operand_aliasing={{0}: (4, {}), {1}: (5, {}), {2}: (6, {})} | custom-call | flops 4294967296 | bytes 20971520 | tf_op jit(solution)/shard_map/pallas_call | solution.py:557
  59.2 1.6 %collective-permute-start.3 = (f32[512,512]{1,0:T(8,128)S(1)}, f32[512,512]{1,0:T(8,128)S(1)}, u32[]{:S(2)}, u32[]{:S(2)}) collective-permute-start(f32[512,512]{1,0:T(8,128)S(1)} %collective-permute-done.2), channel_id=1, source_target_pairs={{4,8},{20,24},{8,4},{24,20},{28,16},{0,12},{5,9},{21,25},{9,5},{25... | collective-permute-start | bytes 3145736 | tf_op jit(solution)/shard_map/ppermute | solution.py:595
  60.8 0.2 shard_map.66.own_ref
  61.1 1.7 %collective-permute-start.6 = (f32[256,128]{1,0:T(8,128)S(1)}, f32[256,128]{1,0:T(8,128)S(1)}, u32[]{:S(2)}, u32[]{:S(2)}) collective-permute-start(f32[256,128]{1,0:T(8,128)S(1)} %shard_map.66.own_ref), channel_id=1, source_target_pairs={{0,1},{1,0},{2,3},{3,2},{4,5},{5,4},{6,7},{7,6},{8,9},{9,8},{10,11... | collective-permute-start | bytes 393224 | tf_op jit(solution)/shard_map/ppermute | solution.py:593
  62.7 5.1 %shard_map.71 = (f32[4,1024,512]{2,1,0:T(8,128)S(1)}, bf16[2048,256]{1,0:T(8,128)(2,1)S(1)}, f8e4m3fn[4096,256]{1,0:T(32,128)(4,1)S(1)}) custom-call(f32[3,1,2048]{2,1,0:T(1,128)S(1)} %bitcast.10, f32[3,2048,128]{2,1,0:T(8,128)S(1)} %get-tuple-element.36.spread_ref, ...), custom_call_target="tpu_custom_call", output_to_operand_aliasing={{0}: (4, {}), {1}: (5, {}), {2}: (6, {})} | custom-call | flops 4294967296 | bytes 20971520 | tf_op jit(solution)/shard_map/pallas_call | solution.py:557
  67.9 0.2 shard_map.67
  68.2 2.6 %collective-permute-start.7 = (f32[256,128]{1,0:T(8,128)S(1)}, f32[256,128]{1,0:T(8,128)S(1)}, u32[]{:S(2)}, u32[]{:S(2)}) collective-permute-start(f32[256,128]{1,0:T(8,128)S(1)} %shard_map.67), channel_id=1, source_target_pairs={{0,2},{1,3},{2,0},{3,1},{4,6},{5,7},{6,4},{7,5},{8,10},{9,11},{10,... | collective-permute-start | bytes 393224 | tf_op jit(solution)/shard_map/ppermute | solution.py:593
  70.8 4.9 %shard_map.72 = (f32[4,1024,512]{2,1,0:T(8,128)S(1)}, bf16[2048,256]{1,0:T(8,128)(2,1)S(1)}, f8e4m3fn[4096,256]{1,0:T(32,128)(4,1)S(1)}) custom-call(f32[3,1,2048]{2,1,0:T(1,128)S(1)} %bitcast.11, f32[3,2048,128]{2,1,0:T(8,128)S(1)} %get-tuple-element.36.spread_ref, ...), custom_call_target="tpu_custom_call", output_to_operand_aliasing={{0}: (4, {}), {1}: (5, {}), {2}: (6, {})} | custom-call | flops 4294967296 | bytes 20971520 | tf_op jit(solution)/shard_map/pallas_call | solution.py:557
  75.7 2.0 %collective-permute-done.7.refs_3_ = f32[256,128]{1,0:T(8,128)S(1)} collective-permute-done((f32[256,128]{1,0:T(8,128)S(1)}, f32[256,128]{1,0:T(8,128)S(1)}, u32[]{:S(2)}, u32[]{:S(2)}) %collective-permute-start.7) | collective-permute-done | bytes 131104 | tf_op jit(solution)/shard_map/ppermute | solution.py:593
  77.7 0.4 shard_map.68.mine_ref
  78.1 0.7 collective-permute-start.8
  78.8 7.4 %middle.1.near_ref = f32[4,1024,512]{2,1,0:T(8,128)S(1)} custom-call(f32[3,1,2048]{2,1,0:T(1,128)S(1)} %bitcast.12, f32[1032,640]{1,0:T(8,128)S(1)} %collective-permute-done.other_ref.core_ref, f32[4,1024,512]{2,1,0:T(8,128)S(1)} %get-tuple-element.46.near_ref), custom_call_target="tpu_custom_call", output_to_operand_aliasing={{}: (2, {})} | custom-call | flops 4294967296 | bytes 16777216 | tf_op jit(solution)/shard_map/middle/pallas_call | solution.py:612
  86.1 0.0 collective-permute-done.3.lower_ref
  86.2 9.3 %final.1 = f32[1024,16,128]{2,1,0:T(8,128)} custom-call(f32[3,1,2048]{2,1,0:T(1,128)S(1)} %bitcast.13, f32[1032,640]{1,0:T(8,128)S(1)} %collective-permute-done.other_ref.core_ref, f32[520,512]{1,0:T(8,128)S(1)} %collective-permute-done.1.upper_ref, f32[512,512]{1,0:T(8,128)S(1)} %collective-permute-done.3.lower_ref, f32[256,128]{1,0:T(8,128)S(1)} %shard_map.68.mine_ref, ...), custom_call_target="tpu_custom_call" | custom-call | flops 4294967296 | bytes 16777216 | tf_op jit(solution)/shard_map/final/pallas_call | solution.py:624
  (15 shorter events, 0.0 us)
Async XLA Ops:
  0.0 0.7 copy-start
  0.7 0.7 copy-start.5
  1.4 8.7 %copy-start.1 = (f32[3,1,1,2048]{3,2,1,0:T(1,128)S(1)}, f32[3,1,1,2048]{3,2,1,0:T(1,128)}, u32[]{:S(2)}) copy-start(f32[3,1,1,2048]{3,2,1,0:T(1,128)} %param.8) | copy-start | bytes 73732
  1.4 8.7 %copy-start.4 = (f32[1,1,64,2048]{3,2,1,0:T(8,128)S(1)}, f32[1,1,64,2048]{3,2,1,0:T(8,128)}, u32[]{:S(2)}) copy-start(f32[1,1,64,2048]{3,2,1,0:T(8,128)} %param.9) | copy-start | bytes 1572868
  1.4 8.7 %copy-start.6 = (s32[1,1,2048]{2,1,0:T(1,128)S(1)}, s32[1,1,2048]{2,1,0:T(1,128)}, u32[]{:S(2)}) copy-start(s32[1,1,2048]{2,1,0:T(1,128)} %param.7) | copy-start | bytes 24580
  15.3 7.9 %copy-start.2 = (f32[5,2,64,64]{3,2,1,0:T(8,128)S(1)}, f32[5,2,64,64]{3,2,1,0:T(8,128)}, u32[]{:S(2)}) copy-start(f32[5,2,64,64]{3,2,1,0:T(8,128)} %transfer_ref.1) | copy-start | bytes 491524
  15.3 7.9 %copy-start.3 = (f32[5,2,64,64]{3,2,1,0:T(8,128)S(1)}, f32[5,2,64,64]{3,2,1,0:T(8,128)}, u32[]{:S(2)}) copy-start(f32[5,2,64,64]{3,2,1,0:T(8,128)} %coupling_ref.1) | copy-start | bytes 491524
  20.4 5.1 %collective-permute-start = (f32[1032,640]{1,0:T(8,128)S(1)}, f32[1032,640]{1,0:T(8,128)S(1)}, u32[]{:S(2)}, u32[]{:S(2)}) collective-permute-start(f32[1032,640]{1,0:T(8,128)S(1)} %core.1.own_ref), channel_id=1, source_target_pairs={{0,4},{4,0},{8,12},{12,8},{16,20},{20,16},{24,28},{28,24},{1,5},{5... | collective-permute-start | bytes 7925768 | tf_op jit(solution)/shard_map/ppermute | solution.py:538
  21.0 38.3 %collective-permute-start.2 = (f32[512,512]{1,0:T(8,128)S(1)}, f32[512,512]{1,0:T(8,128)S(1)}, u32[]{:S(2)}, u32[]{:S(2)}) collective-permute-start(f32[512,512]{1,0:T(8,128)S(1)} %get-tuple-element.31), channel_id=1, source_target_pairs={{12,28},{16,0},{4,4},{8,8},{20,20},{24,24},{13,29},{17,1},{5,5},{9... | collective-permute-start | bytes 3145736 | tf_op jit(solution)/shard_map/ppermute | solution.py:504
  22.2 63.9 %collective-permute-start.1 = (f32[520,512]{1,0:T(8,128)S(1)}, f32[520,512]{1,0:T(8,128)S(1)}, u32[]{:S(2)}, u32[]{:S(2)}) collective-permute-start(f32[520,512]{1,0:T(8,128)S(1)} %get-tuple-element.30), channel_id=1, source_target_pairs={{4,8},{12,16},{20,24},{8,4},{16,12},{24,20},{5,9},{13,17},{21,25},... | collective-permute-start | bytes 3194888 | tf_op jit(solution)/shard_map/ppermute | solution.py:503
  25.8 25.2 %collective-permute-start.4 = (f32[256,128]{1,0:T(8,128)S(1)}, f32[256,128]{1,0:T(8,128)S(1)}, u32[]{:S(2)}, u32[]{:S(2)}) collective-permute-start(f32[256,128]{1,0:T(8,128)S(1)} %shard_map.64.own_ref), channel_id=1, source_target_pairs={{0,8},{4,12},{8,0},{12,4},{16,24},{20,28},{24,16},{28,20},{1,9},{5... | collective-permute-start | bytes 393224 | tf_op jit(solution)/shard_map/ppermute | solution.py:593
  51.3 9.6 %collective-permute-start.5 = (f32[256,128]{1,0:T(8,128)S(1)}, f32[256,128]{1,0:T(8,128)S(1)}, u32[]{:S(2)}, u32[]{:S(2)}) collective-permute-start(f32[256,128]{1,0:T(8,128)S(1)} %shard_map.65.own_ref), channel_id=1, source_target_pairs={{0,16},{4,20},{8,24},{12,28},{16,0},{20,4},{24,8},{28,12},{1,17},{... | collective-permute-start | bytes 393224 | tf_op jit(solution)/shard_map/ppermute | solution.py:593
  59.2 26.9 %collective-permute-start.3 = (f32[512,512]{1,0:T(8,128)S(1)}, f32[512,512]{1,0:T(8,128)S(1)}, u32[]{:S(2)}, u32[]{:S(2)}) collective-permute-start(f32[512,512]{1,0:T(8,128)S(1)} %collective-permute-done.2), channel_id=1, source_target_pairs={{4,8},{20,24},{8,4},{24,20},{28,16},{0,12},{5,9},{21,25},{9,5},{25... | collective-permute-start | bytes 3145736 | tf_op jit(solution)/shard_map/ppermute | solution.py:595
  61.1 6.8 %collective-permute-start.6 = (f32[256,128]{1,0:T(8,128)S(1)}, f32[256,128]{1,0:T(8,128)S(1)}, u32[]{:S(2)}, u32[]{:S(2)}) collective-permute-start(f32[256,128]{1,0:T(8,128)S(1)} %shard_map.66.own_ref), channel_id=1, source_target_pairs={{0,1},{1,0},{2,3},{3,2},{4,5},{5,4},{6,7},{7,6},{8,9},{9,8},{10,11... | collective-permute-start | bytes 393224 | tf_op jit(solution)/shard_map/ppermute | solution.py:593
  68.2 9.5 %collective-permute-start.7 = (f32[256,128]{1,0:T(8,128)S(1)}, f32[256,128]{1,0:T(8,128)S(1)}, u32[]{:S(2)}, u32[]{:S(2)}) collective-permute-start(f32[256,128]{1,0:T(8,128)S(1)} %shard_map.67), channel_id=1, source_target_pairs={{0,2},{1,3},{2,0},{3,1},{4,6},{5,7},{6,4},{7,5},{8,10},{9,11},{10,... | collective-permute-start | bytes 393224 | tf_op jit(solution)/shard_map/ppermute | solution.py:593
  78.1 8.1 %collective-permute-start.8 = (f32[256,128]{1,0:T(8,128)S(1)}, f32[256,128]{1,0:T(8,128)S(1)}, u32[]{:S(2)}, u32[]{:S(2)}) collective-permute-start(f32[256,128]{1,0:T(8,128)S(1)} %shard_map.68.mine_ref), channel_id=1, source_target_pairs={{0,4},{4,0},{8,12},{12,8},{16,20},{20,16},{24,28},{28,24},{1,5},{5... | collective-permute-start | bytes 393224 | tf_op jit(solution)/shard_map/ppermute | solution.py:601

commit v2 on v1

--- a/solution.py
+++ b/solution.py
@@ -78,7 +78,8 @@
         fine_ref[pl.ds(first, ROWS), :] = hit.astype(FINE8)
 
 
-def cross_kernel(unit, order_ref, jitter_ref, x_ref, upper_ref, lower_ref, high_ref, low_ref, sel_ref, sel8_ref, x_buf, sems):
+def cross_kernel(unit, order_hbm, jitter_hbm, x_ref, upper_ref, lower_ref, high_ref, low_ref, *refs):
+    sel_ref, sel8_ref, x_buf, sems, order_ref, jitter_ref, small_sems = refs
     count, points = high_ref.shape
     width = upper_ref.shape[1]
     pieces = points // LANES
@@ -106,9 +107,17 @@
         here = pl.ds(first, size)
         return dot(high_ref[here, :], sel_ref[...]) + dot(low_ref[here, :points], sel8_ref[...]) * (1.0 / LO_UP)
 
+    small = [
+        pltpu.make_async_copy(order_hbm, order_ref, small_sems.at[0]),
+        pltpu.make_async_copy(jitter_hbm, jitter_ref, small_sems.at[1]),
+    ]
+    for copy in small:
+        copy.start()
     for part in range(parts):
         for copy in copies(part):
             copy.start()
+    for copy in small:
+        copy.wait()
     half = count // 2
     fill_selector(strip_indices(order_ref, tail, width), sel_ref, sel8_ref)
     upper_ref[half:, :] = stack_rows(strip_places(jitter_ref, tail, width, unit), 8)
@@ -473,7 +482,7 @@
     parts = 4
     upper, lower, high, low = pl.pallas_call(
         functools.partial(cross_kernel, unit),
-        in_specs=[vmem, vmem, pl.BlockSpec(memory_space=pltpu.HBM)],
+        in_specs=[pl.BlockSpec(memory_space=pltpu.HBM)] * 3,
         out_specs=[vmem] * 4,
         out_shape=[
             shape((half + 8, width)),
@@ -486,11 +495,14 @@
             pltpu.VMEM((points, width), FINE8),
             pltpu.VMEM((parts, pieces, count // parts, LANES), F32),
             pltpu.SemaphoreType.DMA((parts, pieces)),
+            pltpu.VMEM((1, points), jnp.int32),
+            pltpu.VMEM((3, 1, points), F32),
+            pltpu.SemaphoreType.DMA((2,)),
         ],
         compiler_params=params(20),
         cost_estimate=cost(3 * count * points * width, 16 * count * points),
         name="cross",
-    )(order, offsets, in_hbm(x))
+    )(in_hbm(order), in_hbm(offsets), in_hbm(x))
     last = leaf_count - 1
     middle = leaf_count // 2
     up_pairs = [(i, i + 1) for i in range(1, last, 2)]

time: 95.9 us -> 95.9 us (level)
  Pallas kernels: 59.1 us -> 60.6 us
  local copies, waits for them, and re-layouts: 1.46 us -> 0.02 us
    pallas_call x1, Pallas kernels: 8.69 us -> 10.2 us  [body(): pl.pallas_call(functools.partial(cross_kernel, unit), in_specs=[pl.BlockS...]
    unnamed x14 -> x10, local copies, waits for them, and re-layouts: 1.46 us -> 0.02 us
where the time goes in v2:
time: 95.9 us; the launch traced here: 95.7 us
  Pallas kernels  60.6 us (63%)
  waiting for transfers between devices  19.5 us (20%)
  starting transfers between devices  15.1 us (16%)
    pallas_call x4, Pallas kernels, own(): pl.pallas_call(functools.partial(own_kernel, unit, chunk), in_specs=[vmem...  21.5 us
    ppermute x4, waiting for transfers between devices, body(): siblings.append(lax.ppermute(current, axis, pairs))  17.9 us
    pallas_call x1, Pallas kernels, body(): pl.pallas_call(functools.partial(cross_kernel, unit), in_specs=[pl.BlockS...  10.2 us
    ppermute x4, starting transfers between devices, body(): siblings.append(lax.ppermute(current, axis, pairs))  10.1 us
    pallas_call x1, Pallas kernels, body(): pl.pallas_call(functools.partial(final_kernel, unit), in_specs=[vmem] * 9...  9.27 us
    pallas_call x1, Pallas kernels, body(): pl.pallas_call(functools.partial(middle_kernel, unit), in_specs=[vmem] *...  7.36 us
    pallas_call x1, Pallas kernels, body(): pl.pallas_call(functools.partial(core_kernel, unit), in_specs=[vmem] * 6,...  5.1 us
    pallas_call x1, Pallas kernels, body(): pl.pallas_call(functools.partial(places_kernel, unit), grid=(points // GR...  5.09 us
  transfers between devices with their start and end apart: 9, of which 3 were waited for; matrix products, arithmetic and copies ran while one was open for 0% of the time, Pallas kernels for 32%

profile of v2, /device:TPU:0, one launch (start us, length us, event | category | flops | bytes accessed | tf_op | source)
XLA Modules:
  0.0 95.7 jit_solution(15422297944346655454)
XLA Ops:
  0.0 10.2 %cross.1 = (f32[520,512]{1,0:T(8,128)S(1)}, f32[512,512]{1,0:T(8,128)S(1)}, bf16[1024,2048]{1,0:T(8,128)(2,1)S(1)}, f8e5m2[1024,4096]{1,0:T(32,128)(4,1)S(1)}) custom-call(s32[1,2048]{1,0:T(1,128)} %bitcast.15, f32[3,1,2048]{2,1,0:T(1,128)} %bitcast.5, f32[1024,16,128]{2,1,0:T(8,128)} %bitcast.18), custom_call_target="tpu_custom_call" | custom-call | flops 3221225472 | bytes 33554432 | tf_op jit(solution)/shard_map/cross/pallas_call | solution.py:483
  10.3 5.1 %places.1 = (f32[3,2048,128]{2,1,0:T(8,128)S(1)}, bf16[2048,256]{1,0:T(8,128)(2,1)S(1)}, f8e4m3fn[2048,128]{1,0:T(32,128)(4,1)S(1)}, bf16[256,2048]{1,0:T(8,128)(2,1)S(1)}) custom-call(s32[1,2048]{1,0:T(1,128)S(1)} %bitcast.16, f32[3,1,2048]{2,1,0:T(1,128)S(1)} %bitcast.6, f32[64,2048]{1,0:T(8,128)S(1)} %bitcast.14), custom_call_target="tpu_custom_call" | custom-call | flops 2147483648 | bytes 10485760 | tf_op jit(solution)/shard_map/places/pallas_call | solution.py:518
  15.4 0.0 copy-start.1
  15.4 0.0 copy-start.2
  15.4 5.1 %core.1.own_ref = f32[1032,640]{1,0:T(8,128)S(1)} custom-call(s32[1,2048]{1,0:T(1,128)S(1)} %bitcast.17, f32[3,1,2048]{2,1,0:T(1,128)S(1)} %bitcast.7, bf16[2048,256]{1,0:T(8,128)(2,1)S(1)} %get-tuple-element.26.base16_ref, f8e4m3fn[2048,128]{1,0:T(32,128)(4,1)S(1)} %get-tuple-element.27.base8_ref, bf16[1024,2048]{1,0:T(8,128)(2,1)S(1)} %get-tuple-element.28.high_ref, ...), custom_call_target="tpu_custom_call" | custom-call | flops 4831838208 | bytes 12582912 | tf_op jit(solution)/shard_map/core/pallas_call | solution.py:540
  20.5 0.6 collective-permute-start
  21.1 1.3 %collective-permute-start.2 = (f32[512,512]{1,0:T(8,128)S(1)}, f32[512,512]{1,0:T(8,128)S(1)}, u32[]{:S(2)}, u32[]{:S(2)}) collective-permute-start(f32[512,512]{1,0:T(8,128)S(1)} %get-tuple-element.31), channel_id=1, source_target_pairs={{12,28},{16,0},{4,4},{8,8},{20,20},{24,24},{13,29},{17,1},{5,5},{9... | collective-permute-start | bytes 3145736 | tf_op jit(solution)/shard_map/ppermute | solution.py:516
  22.4 0.9 collective-permute-start.1
  23.3 0.8 matrices.1
  24.1 1.6 %collective-permute-done.other_ref.core_ref = f32[1032,640]{1,0:T(8,128)S(1)} collective-permute-done((f32[1032,640]{1,0:T(8,128)S(1)}, f32[1032,640]{1,0:T(8,128)S(1)}, u32[]{:S(2)}, u32[]{:S(2)}) %collective-permute-start) | collective-permute-done | bytes 2641952 | tf_op jit(solution)/shard_map/ppermute | solution.py:550
  25.6 0.2 shard_map.64.own_ref
  25.9 2.9 %collective-permute-start.4 = (f32[256,128]{1,0:T(8,128)S(1)}, f32[256,128]{1,0:T(8,128)S(1)}, u32[]{:S(2)}, u32[]{:S(2)}) collective-permute-start(f32[256,128]{1,0:T(8,128)S(1)} %shard_map.64.own_ref), channel_id=1, source_target_pairs={{0,8},{4,12},{8,0},{12,4},{16,24},{20,28},{24,16},{28,20},{1,9},{5... | collective-permute-start | bytes 393224 | tf_op jit(solution)/shard_map/ppermute | solution.py:605
  28.8 6.3 %shard_map.69 = (f32[4,1024,512]{2,1,0:T(8,128)S(1)}, bf16[2048,256]{1,0:T(8,128)(2,1)S(1)}, f8e4m3fn[4096,256]{1,0:T(32,128)(4,1)S(1)}) custom-call(f32[3,1,2048]{2,1,0:T(1,128)S(1)} %bitcast.8, f32[3,2048,128]{2,1,0:T(8,128)S(1)} %get-tuple-element.36.spread_ref, bf16[1024,2048]{1,0:T(8,128)(2,1)S(1)} %get-tuple-element.28.high_ref, ...), custom_call_target="tpu_custom_call" | custom-call | flops 4294967296 | bytes 20971520 | tf_op jit(solution)/shard_map/pallas_call | solution.py:569
  35.1 16.0 %collective-permute-done.4.other_ref.refs_0_ = f32[256,128]{1,0:T(8,128)S(1)} collective-permute-done((f32[256,128]{1,0:T(8,128)S(1)}, f32[256,128]{1,0:T(8,128)S(1)}, u32[]{:S(2)}, u32[]{:S(2)}) %collective-permute-start.4) | collective-permute-done | bytes 131104 | tf_op jit(solution)/shard_map/ppermute | solution.py:605
  51.1 0.3 shard_map.65.own_ref
  51.3 2.9 %collective-permute-start.5 = (f32[256,128]{1,0:T(8,128)S(1)}, f32[256,128]{1,0:T(8,128)S(1)}, u32[]{:S(2)}, u32[]{:S(2)}) collective-permute-start(f32[256,128]{1,0:T(8,128)S(1)} %shard_map.65.own_ref), channel_id=1, source_target_pairs={{0,16},{4,20},{8,24},{12,28},{16,0},{20,4},{24,8},{28,12},{1,17},{... | collective-permute-start | bytes 393224 | tf_op jit(solution)/shard_map/ppermute | solution.py:605
  54.2 5.1 %shard_map.70 = (f32[4,1024,512]{2,1,0:T(8,128)S(1)}, bf16[2048,256]{1,0:T(8,128)(2,1)S(1)}, f8e4m3fn[4096,256]{1,0:T(32,128)(4,1)S(1)}) custom-call(f32[3,1,2048]{2,1,0:T(1,128)S(1)} %bitcast.9, f32[3,2048,128]{2,1,0:T(8,128)S(1)} %get-tuple-element.36.spread_ref, ...), custom_call_target="tpu_custom_call", output_to_operand_aliasing={{0}: (4, {}), {1}: (5, {}), {2}: (6, {})} | custom-call | flops 4294967296 | bytes 20971520 | tf_op jit(solution)/shard_map/pallas_call | solution.py:569
  59.4 1.6 %collective-permute-start.3 = (f32[512,512]{1,0:T(8,128)S(1)}, f32[512,512]{1,0:T(8,128)S(1)}, u32[]{:S(2)}, u32[]{:S(2)}) collective-permute-start(f32[512,512]{1,0:T(8,128)S(1)} %collective-permute-done.2), channel_id=1, source_target_pairs={{4,8},{20,24},{8,4},{24,20},{28,16},{0,12},{5,9},{21,25},{9,5},{25... | collective-permute-start | bytes 3145736 | tf_op jit(solution)/shard_map/ppermute | solution.py:607
  60.9 0.0 collective-permute-done.5.other_ref.refs_1_
  61.0 0.2 shard_map.66.own_ref
  61.2 1.6 %collective-permute-start.6 = (f32[256,128]{1,0:T(8,128)S(1)}, f32[256,128]{1,0:T(8,128)S(1)}, u32[]{:S(2)}, u32[]{:S(2)}) collective-permute-start(f32[256,128]{1,0:T(8,128)S(1)} %shard_map.66.own_ref), channel_id=1, source_target_pairs={{0,1},{1,0},{2,3},{3,2},{4,5},{5,4},{6,7},{7,6},{8,9},{9,8},{10,11... | collective-permute-start | bytes 393224 | tf_op jit(solution)/shard_map/ppermute | solution.py:605
  62.8 5.1 %shard_map.71 = (f32[4,1024,512]{2,1,0:T(8,128)S(1)}, bf16[2048,256]{1,0:T(8,128)(2,1)S(1)}, f8e4m3fn[4096,256]{1,0:T(32,128)(4,1)S(1)}) custom-call(f32[3,1,2048]{2,1,0:T(1,128)S(1)} %bitcast.10, f32[3,2048,128]{2,1,0:T(8,128)S(1)} %get-tuple-element.36.spread_ref, ...), custom_call_target="tpu_custom_call", output_to_operand_aliasing={{0}: (4, {}), {1}: (5, {}), {2}: (6, {})} | custom-call | flops 4294967296 | bytes 20971520 | tf_op jit(solution)/shard_map/pallas_call | solution.py:569
  68.0 0.0 collective-permute-done.6.other_ref.refs_2_
  68.0 0.2 shard_map.67
  68.3 2.7 %collective-permute-start.7 = (f32[256,128]{1,0:T(8,128)S(1)}, f32[256,128]{1,0:T(8,128)S(1)}, u32[]{:S(2)}, u32[]{:S(2)}) collective-permute-start(f32[256,128]{1,0:T(8,128)S(1)} %shard_map.67), channel_id=1, source_target_pairs={{0,2},{1,3},{2,0},{3,1},{4,6},{5,7},{6,4},{7,5},{8,10},{9,11},{10,... | collective-permute-start | bytes 393224 | tf_op jit(solution)/shard_map/ppermute | solution.py:605
  70.9 4.9 %shard_map.72 = (f32[4,1024,512]{2,1,0:T(8,128)S(1)}, bf16[2048,256]{1,0:T(8,128)(2,1)S(1)}, f8e4m3fn[4096,256]{1,0:T(32,128)(4,1)S(1)}) custom-call(f32[3,1,2048]{2,1,0:T(1,128)S(1)} %bitcast.11, f32[3,2048,128]{2,1,0:T(8,128)S(1)} %get-tuple-element.36.spread_ref, ...), custom_call_target="tpu_custom_call", output_to_operand_aliasing={{0}: (4, {}), {1}: (5, {}), {2}: (6, {})} | custom-call | flops 4294967296 | bytes 20971520 | tf_op jit(solution)/shard_map/pallas_call | solution.py:569
  75.8 2.0 %collective-permute-done.7.refs_3_ = f32[256,128]{1,0:T(8,128)S(1)} collective-permute-done((f32[256,128]{1,0:T(8,128)S(1)}, f32[256,128]{1,0:T(8,128)S(1)}, u32[]{:S(2)}, u32[]{:S(2)}) %collective-permute-start.7) | collective-permute-done | bytes 131104 | tf_op jit(solution)/shard_map/ppermute | solution.py:605
  77.8 0.4 shard_map.68.mine_ref
  78.2 0.7 collective-permute-start.8
  78.8 7.4 %middle.1.near_ref = f32[4,1024,512]{2,1,0:T(8,128)S(1)} custom-call(f32[3,1,2048]{2,1,0:T(1,128)S(1)} %bitcast.12, f32[1032,640]{1,0:T(8,128)S(1)} %collective-permute-done.other_ref.core_ref, f32[4,1024,512]{2,1,0:T(8,128)S(1)} %get-tuple-element.46.near_ref), custom_call_target="tpu_custom_call", output_to_operand_aliasing={{}: (2, {})} | custom-call | flops 4294967296 | bytes 16777216 | tf_op jit(solution)/shard_map/middle/pallas_call | solution.py:624
  86.2 0.0 collective-permute-done.3.lower_ref
  86.2 9.3 %final.1 = f32[1024,16,128]{2,1,0:T(8,128)} custom-call(f32[3,1,2048]{2,1,0:T(1,128)S(1)} %bitcast.13, f32[1032,640]{1,0:T(8,128)S(1)} %collective-permute-done.other_ref.core_ref, f32[520,512]{1,0:T(8,128)S(1)} %collective-permute-done.1.upper_ref, f32[512,512]{1,0:T(8,128)S(1)} %collective-permute-done.3.lower_ref, f32[256,128]{1,0:T(8,128)S(1)} %shard_map.68.mine_ref, ...), custom_call_target="tpu_custom_call" | custom-call | flops 4294967296 | bytes 16777216 | tf_op jit(solution)/shard_map/final/pallas_call | solution.py:636
  (11 shorter events, 0.0 us)
Async XLA Ops:
  0.0 10.3 %copy-start = (f32[3,1,1,2048]{3,2,1,0:T(1,128)S(1)}, f32[3,1,1,2048]{3,2,1,0:T(1,128)}, u32[]{:S(2)}) copy-start(f32[3,1,1,2048]{3,2,1,0:T(1,128)} %param.8) | copy-start | bytes 73732
  0.0 10.3 %copy-start.4 = (s32[1,1,2048]{2,1,0:T(1,128)S(1)}, s32[1,1,2048]{2,1,0:T(1,128)}, u32[]{:S(2)}) copy-start(s32[1,1,2048]{2,1,0:T(1,128)} %param.7) | copy-start | bytes 24580
  0.0 10.3 %copy-start.3 = (f32[1,1,64,2048]{3,2,1,0:T(8,128)S(1)}, f32[1,1,64,2048]{3,2,1,0:T(8,128)}, u32[]{:S(2)}) copy-start(f32[1,1,64,2048]{3,2,1,0:T(8,128)} %param.9) | copy-start | bytes 1572868
  15.4 7.9 %copy-start.1 = (f32[5,2,64,64]{3,2,1,0:T(8,128)S(1)}, f32[5,2,64,64]{3,2,1,0:T(8,128)}, u32[]{:S(2)}) copy-start(f32[5,2,64,64]{3,2,1,0:T(8,128)} %transfer_ref.1) | copy-start | bytes 491524
  15.4 7.9 %copy-start.2 = (f32[5,2,64,64]{3,2,1,0:T(8,128)S(1)}, f32[5,2,64,64]{3,2,1,0:T(8,128)}, u32[]{:S(2)}) copy-start(f32[5,2,64,64]{3,2,1,0:T(8,128)} %coupling_ref.1) | copy-start | bytes 491524
  20.5 5.1 %collective-permute-start = (f32[1032,640]{1,0:T(8,128)S(1)}, f32[1032,640]{1,0:T(8,128)S(1)}, u32[]{:S(2)}, u32[]{:S(2)}) collective-permute-start(f32[1032,640]{1,0:T(8,128)S(1)} %core.1.own_ref), channel_id=1, source_target_pairs={{0,4},{4,0},{8,12},{12,8},{16,20},{20,16},{24,28},{28,24},{1,5},{5... | collective-permute-start | bytes 7925768 | tf_op jit(solution)/shard_map/ppermute | solution.py:550
  21.1 38.3 %collective-permute-start.2 = (f32[512,512]{1,0:T(8,128)S(1)}, f32[512,512]{1,0:T(8,128)S(1)}, u32[]{:S(2)}, u32[]{:S(2)}) collective-permute-start(f32[512,512]{1,0:T(8,128)S(1)} %get-tuple-element.31), channel_id=1, source_target_pairs={{12,28},{16,0},{4,4},{8,8},{20,20},{24,24},{13,29},{17,1},{5,5},{9... | collective-permute-start | bytes 3145736 | tf_op jit(solution)/shard_map/ppermute | solution.py:516
  22.4 63.8 %collective-permute-start.1 = (f32[520,512]{1,0:T(8,128)S(1)}, f32[520,512]{1,0:T(8,128)S(1)}, u32[]{:S(2)}, u32[]{:S(2)}) collective-permute-start(f32[520,512]{1,0:T(8,128)S(1)} %get-tuple-element.30), channel_id=1, source_target_pairs={{4,8},{12,16},{20,24},{8,4},{16,12},{24,20},{5,9},{13,17},{21,25},... | collective-permute-start | bytes 3194888 | tf_op jit(solution)/shard_map/ppermute | solution.py:515
  25.9 25.2 %collective-permute-start.4 = (f32[256,128]{1,0:T(8,128)S(1)}, f32[256,128]{1,0:T(8,128)S(1)}, u32[]{:S(2)}, u32[]{:S(2)}) collective-permute-start(f32[256,128]{1,0:T(8,128)S(1)} %shard_map.64.own_ref), channel_id=1, source_target_pairs={{0,8},{4,12},{8,0},{12,4},{16,24},{20,28},{24,16},{28,20},{1,9},{5... | collective-permute-start | bytes 393224 | tf_op jit(solution)/shard_map/ppermute | solution.py:605
  51.3 9.6 %collective-permute-start.5 = (f32[256,128]{1,0:T(8,128)S(1)}, f32[256,128]{1,0:T(8,128)S(1)}, u32[]{:S(2)}, u32[]{:S(2)}) collective-permute-start(f32[256,128]{1,0:T(8,128)S(1)} %shard_map.65.own_ref), channel_id=1, source_target_pairs={{0,16},{4,20},{8,24},{12,28},{16,0},{20,4},{24,8},{28,12},{1,17},{... | collective-permute-start | bytes 393224 | tf_op jit(solution)/shard_map/ppermute | solution.py:605
  59.4 26.8 %collective-permute-start.3 = (f32[512,512]{1,0:T(8,128)S(1)}, f32[512,512]{1,0:T(8,128)S(1)}, u32[]{:S(2)}, u32[]{:S(2)}) collective-permute-start(f32[512,512]{1,0:T(8,128)S(1)} %collective-permute-done.2), channel_id=1, source_target_pairs={{4,8},{20,24},{8,4},{24,20},{28,16},{0,12},{5,9},{21,25},{9,5},{25... | collective-permute-start | bytes 3145736 | tf_op jit(solution)/shard_map/ppermute | solution.py:607
  61.2 6.8 %collective-permute-start.6 = (f32[256,128]{1,0:T(8,128)S(1)}, f32[256,128]{1,0:T(8,128)S(1)}, u32[]{:S(2)}, u32[]{:S(2)}) collective-permute-start(f32[256,128]{1,0:T(8,128)S(1)} %shard_map.66.own_ref), channel_id=1, source_target_pairs={{0,1},{1,0},{2,3},{3,2},{4,5},{5,4},{6,7},{7,6},{8,9},{9,8},{10,11... | collective-permute-start | bytes 393224 | tf_op jit(solution)/shard_map/ppermute | solution.py:605
  68.3 9.5 %collective-permute-start.7 = (f32[256,128]{1,0:T(8,128)S(1)}, f32[256,128]{1,0:T(8,128)S(1)}, u32[]{:S(2)}, u32[]{:S(2)}) collective-permute-start(f32[256,128]{1,0:T(8,128)S(1)} %shard_map.67), channel_id=1, source_target_pairs={{0,2},{1,3},{2,0},{3,1},{4,6},{5,7},{6,4},{7,5},{8,10},{9,11},{10,... | collective-permute-start | bytes 393224 | tf_op jit(solution)/shard_map/ppermute | solution.py:605
  78.2 8.0 %collective-permute-start.8 = (f32[256,128]{1,0:T(8,128)S(1)}, f32[256,128]{1,0:T(8,128)S(1)}, u32[]{:S(2)}, u32[]{:S(2)}) collective-permute-start(f32[256,128]{1,0:T(8,128)S(1)} %shard_map.68.mine_ref), channel_id=1, source_target_pairs={{0,4},{4,0},{8,12},{12,8},{16,20},{20,16},{24,28},{28,24},{1,5},{5... | collective-permute-start | bytes 393224 | tf_op jit(solution)/shard_map/ppermute | solution.py:613
